TPU v7x, 512 devices: a whole 4x8x8 slice. The times are simulated.
512 devices in a mesh: tm: 256 (over x_lo, z, y, core), space: 2 (over x_hi).
Axes of the slice: x: 4 (x_hi: 2, x_lo: 2; x = x_hi * 2 + x_lo), y: 8, z: 8, core: 2. Of those that a mesh axis runs over, the one named last changes fastest.
Arguments:
- control: float32 [32, 512], P('space'), may hold values from -0.6 to 0.6
- initial: float32 [32, 512], P('space'), may hold values from -6 to 6
- diffusion: float32 [32, 512], P('space'), may hold values from 0.1 to 1
- reaction: float32 [32, 512], P('space'), may hold values from 4.8828124e-06 to 0.1
- forward_guess: float32 [256, 32, 512], P('tm', 'space'), may hold values from -1.5 to 1.5
- adjoint_guess: float32 [256, 32, 512], P('tm', 'space'), may hold values from -1.5 to 1.5
- observed: float32 [256, 32, 512], P('tm', 'space'), may hold values from -6 to 6
Outputs:
- forward_states: float32 [256, 32, 512], P('tm', 'space')
- adjoint_states: float32 [256, 32, 512], P('tm', 'space')
- control_gradient: float32 [32, 512], P('space')
All inputs are finite; a program needn't handle non-finite values.
Results may differ from a plain program's by a relative error of at most 0.00015.
Values sent between devices are 32-bit elements; how exact they have to be, the bound alone decides.
No kernel may reach another device: no remote copies, remote signals or barrier semaphores. Data moves between devices by JAX's collectives and lax.ppermute only.
A program may use at most 128 MiB of HBM per device.

v0:
```python
import functools

import jax
import jax.numpy as jnp
from jax import lax
from jax.sharding import Mesh
from jax.sharding import PartitionSpec as P

SWEEPS = 3
COARSEN = 8
TM = ("tm_0", "tm_1", "tm_2", "tm_3")


def with_halo(value, sides, width):
    for axis, dim in sides:
        size, length = (lax.axis_size(axis), value.shape[dim])
        up = [(i, (i + 1) % size) for i in range(size - 1)]
        down = [(j, i) for i, j in up]
        last = lax.slice_in_dim(value, length - width, length, axis=dim)
        leading = lax.slice_in_dim(value, 0, width, axis=dim)
        before = lax.ppermute(last, axis, up)
        after = lax.ppermute(leading, axis, down)
        value = jnp.concatenate([before, value, after], axis=dim)
    return value


def passed_along(block, axis, distance):
    devices = range(lax.axis_size(axis))
    route = [(i - distance, i) for i in devices if i - distance in devices]
    return lax.ppermute(block, axis, route)


def neutral_like(value, identity):
    return jax.tree.map(
        lambda a, e: jnp.broadcast_to(jnp.asarray(e, a.dtype), a.shape), value, identity
    )


def all_in_one(value, axis):
    leaves = jax.tree.leaves(value)
    sequence = sorted(range(len(leaves)), key=lambda k: -leaves[k].size)
    width = (1, *leaves[sequence[0]].shape)[-1]
    lines = [
        jnp.pad(leaves[k].reshape(-1), (0, -leaves[k].size % width)).reshape(-1, width)
        for k in sequence
    ]
    both, at, found = (lax.all_gather(jnp.concatenate(lines), axis), 0, {})
    for k, line in zip(sequence, lines):
        share = both[:, at : at + len(line)].reshape(len(both), -1)
        found[k] = share[:, : leaves[k].size].reshape(-1, *leaves[k].shape)
        at += len(line)
    numbers = iter(range(len(leaves)))
    return jax.tree.map(lambda _: found[next(numbers)], value)


def entering(value, axes, combine, identity, reverse):
    before = start = neutral_like(value, identity)
    total = value
    for axis in reversed(axes):
        length, here = (lax.axis_size(axis), lax.axis_index(axis))
        pieces = all_in_one(total, axis)
        inside, total = (start, start)
        for k in reversed(range(length)) if reverse else range(length):
            passed = k > here if reverse else k < here
            total = combine(total, jax.tree.map(lambda part: part[k], pieces))
            inside = jax.tree.map(lambda new, old: jnp.where(passed, new, old), total, inside)
        before = combine(inside, before)
    return before


def by_axis(value, axes):
    return functools.reduce(lax.psum, axes, value)


def neighbours(source):
    zero_row = jnp.zeros_like(source[..., :1, :])
    zero_column = jnp.zeros_like(source[..., :, :1])
    vertical = jnp.concatenate([source[..., 1:, :], zero_row], -2) + jnp.concatenate(
        [zero_row, source[..., :-1, :]], -2
    )
    lateral = jnp.concatenate([source[..., :, 1:], zero_column], -1) + jnp.concatenate(
        [zero_column, source[..., :, :-1]], -1
    )
    return vertical + lateral


def forward_step(previous, control, spread, diagonal):
    padded = with_halo(previous + control, (("space", 0),), SWEEPS)
    iterate = padded
    for number in range(SWEEPS):
        iterate = (padded + spread * neighbours(iterate)) / diagonal
    return iterate[SWEEPS : SWEEPS + previous.shape[0]]


def adjoint_step(following, misfit, weight, diagonal):
    padded = with_halo(following + misfit, (("space", 0),), SWEEPS)
    carried = padded
    summed = padded
    for number in range(SWEEPS - 1):
        carried = neighbours(weight * carried)
        summed = summed + carried
    result = summed / diagonal + neighbours(weight * carried)
    return result[SWEEPS : SWEEPS + following.shape[0]]


def entries(own_forward, own_adjoint, initial):
    arriving = passed_along(own_forward, TM, 1)
    entry_forward = jnp.where(lax.axis_index(TM) == 0, initial, arriving)
    entry_adjoint = passed_along(own_adjoint, TM, -1)
    return (entry_forward, entry_adjoint)


def relax(own_forward, own_adjoint, initial, control, target, spread, weight, diagonal, first_pass):
    entry_forward, entry_adjoint = entries(own_forward, own_adjoint, initial)
    states = []
    current = entry_forward
    for number in range(COARSEN - 1):
        current = forward_step(current, control, spread, diagonal)
        states.append(current)
    points = states + [own_forward]
    current = entry_adjoint
    fine_total = jnp.zeros_like(own_adjoint)
    for position in range(COARSEN, 1, -1):
        misfit = (points[position - 1] - target) / COARSEN
        current = adjoint_step(current, misfit, weight, diagonal)
        fine_total = fine_total + current
    if first_pass:
        forward_residual = forward_step(states[-1], control, spread, diagonal) - own_forward
        adjoint_residual = (
            adjoint_step(current, (points[0] - target) / COARSEN, weight, diagonal) - own_adjoint
        )
        return (forward_residual, adjoint_residual)
    return fine_total


def compose(earlier, latter):
    return (earlier[0] * latter[0], latter[0] * earlier[1] + latter[1])


def shards(control, initial, diffusion, reaction, forward_guess, adjoint_guess, observed):
    coefficients = with_halo(jnp.stack((diffusion, reaction)), (("space", 1),), SWEEPS)
    spread = coefficients[0]
    diagonal = 1.0 + 4.0 * spread + coefficients[1]
    weight = spread / diagonal
    own_forward = forward_guess[0]
    own_adjoint = adjoint_guess[0]
    target = observed[0]
    forward_residual, adjoint_residual = relax(
        own_forward, own_adjoint, initial, control, target, spread, weight, diagonal, True
    )
    damping = 1.0 / (1.0 + COARSEN * reaction)
    unit_field = jnp.ones_like(damping)
    zero_field = jnp.zeros_like(damping)
    prior_pair = entering((damping, forward_residual), TM, compose, (unit_field, zero_field), False)
    later_pair = entering((damping, adjoint_residual), TM, compose, (unit_field, zero_field), True)
    forward_correction = damping * prior_pair[1] + forward_residual
    adjoint_correction = damping * later_pair[1] + adjoint_residual
    forward_states = own_forward + forward_correction
    adjoint_states = own_adjoint + adjoint_correction
    steps_total = COARSEN * lax.axis_size(TM)
    fine_local = relax(
        forward_states, adjoint_states, initial, control, target, spread, weight, diagonal, False
    )
    gradient = by_axis(adjoint_states + fine_local, TM) / steps_total
    return (forward_states[None], adjoint_states[None], gradient)


def solution(mesh):
    finer = Mesh(
        mesh.devices.reshape(2, 8, 8, 2, mesh.shape["space"]),
        ("tm_0", "tm_1", "tm_2", "tm_3", "space"),
    )
    return jax.shard_map(
        shards,
        mesh=finer,
        in_specs=(
            P("space", None),
            P("space", None),
            P("space", None),
            P("space", None),
            P(TM, "space", None),
            P(TM, "space", None),
            P(TM, "space", None),
        ),
        out_specs=(P(TM, "space", None), P(TM, "space", None), P("space", None)),
        check_vma=False,
    )
```

profile of v0, /device:TPU:6, one launch (start us, length us, event | category | flops | bytes accessed | tf_op | source)
XLA Modules:
  0.0 491.6 jit_solution(17753908857167367100)
XLA Ops:
  6.1 12.4 %collective-permute-start.19 = (f32[16,512]{1,0:T(8,128)S(1)}, f32[16,512]{1,0:T(8,128)S(1)}, u32[]{:S(2)}, u32[]{:S(2)}) collective-permute-start(f32[16,512]{1,0:T(8,128)S(1)} %bitcast.959), channel_id=1, source_target_pairs={{2,0},{4,2},{6,4},{8,6},{10,8},{12,10},{14,12},{16,14},{18,16},{20... | collective-permute-start | bytes 98312 | tf_op jit(solution)/shard_map/ppermute | solution.py:30
  21.3 6.4 %collective-permute-start.21 = (f32[3,512]{1,0:T(4,128)S(1)}, f32[3,512]{1,0:T(4,128)S(1)}, u32[]{:S(2)}, u32[]{:S(2)}) collective-permute-start(f32[3,512]{1,0:T(4,128)S(1)} %get-tuple-element.578), channel_id=1, source_target_pairs={{1,0},{3,2},{5,4},{7,6},{9,8},{11,10},{13,12},{15,14},{17,16},{19,... | collective-permute-start | bytes 18440 | tf_op jit(solution)/shard_map/ppermute | solution.py:22
  29.0 6.0 %collective-permute-start.2 = (f32[3,512]{1,0:T(4,128)S(1)}, f32[3,512]{1,0:T(4,128)S(1)}, u32[]{:S(2)}, u32[]{:S(2)}) collective-permute-start(f32[3,512]{1,0:T(4,128)S(1)} %get-tuple-element.576), channel_id=1, source_target_pairs={{1,0},{3,2},{5,4},{7,6},{9,8},{11,10},{13,12},{15,14},{17,16},{19,... | collective-permute-start | bytes 18440 | tf_op jit(solution)/shard_map/ppermute | solution.py:22
  55.1 5.7 %collective-permute-done.7 = f32[3,512]{1,0:T(4,128)S(1)} collective-permute-done((f32[3,512]{1,0:T(4,128)S(1)}, f32[3,512]{1,0:T(4,128)S(1)}, u32[]{:S(2)}, u32[]{:S(2)}) %collective-permute-start.7) | collective-permute-done | bytes 6176 | tf_op jit(solution)/shard_map/ppermute | solution.py:21
  64.3 5.7 %collective-permute-done.9 = f32[3,512]{1,0:T(4,128)S(1)} collective-permute-done((f32[3,512]{1,0:T(4,128)S(1)}, f32[3,512]{1,0:T(4,128)S(1)}, u32[]{:S(2)}, u32[]{:S(2)}) %collective-permute-start.9) | collective-permute-done | bytes 6176 | tf_op jit(solution)/shard_map/ppermute | solution.py:21
  83.0 5.7 %collective-permute-done.13 = f32[3,512]{1,0:T(4,128)S(1)} collective-permute-done((f32[3,512]{1,0:T(4,128)S(1)}, f32[3,512]{1,0:T(4,128)S(1)}, u32[]{:S(2)}, u32[]{:S(2)}) %collective-permute-start.13) | collective-permute-done | bytes 6176 | tf_op jit(solution)/shard_map/ppermute | solution.py:21
  92.2 5.7 %collective-permute-done.15 = f32[3,512]{1,0:T(4,128)S(1)} collective-permute-done((f32[3,512]{1,0:T(4,128)S(1)}, f32[3,512]{1,0:T(4,128)S(1)}, u32[]{:S(2)}, u32[]{:S(2)}) %collective-permute-start.15) | collective-permute-done | bytes 6176 | tf_op jit(solution)/shard_map/ppermute | solution.py:21
  101.5 6.0 %collective-permute-start.23 = (f32[3,512]{1,0:T(4,128)S(1)}, f32[3,512]{1,0:T(4,128)S(1)}, u32[]{:S(2)}, u32[]{:S(2)}) collective-permute-start(f32[3,512]{1,0:T(4,128)S(1)} %get-tuple-element.562), channel_id=1, source_target_pairs={{1,0},{3,2},{5,4},{7,6},{9,8},{11,10},{13,12},{15,14},{17,16},{19,... | collective-permute-start | bytes 18440 | tf_op jit(solution)/shard_map/ppermute | solution.py:22
  118.2 5.7 %collective-permute-done.24 = f32[3,512]{1,0:T(4,128)S(1)} collective-permute-done((f32[3,512]{1,0:T(4,128)S(1)}, f32[3,512]{1,0:T(4,128)S(1)}, u32[]{:S(2)}, u32[]{:S(2)}) %collective-permute-start.24) | collective-permute-done | bytes 6176 | tf_op jit(solution)/shard_map/ppermute | solution.py:21
  127.5 5.7 %collective-permute-done.26 = f32[3,512]{1,0:T(4,128)S(1)} collective-permute-done((f32[3,512]{1,0:T(4,128)S(1)}, f32[3,512]{1,0:T(4,128)S(1)}, u32[]{:S(2)}, u32[]{:S(2)}) %collective-permute-start.26) | collective-permute-done | bytes 6176 | tf_op jit(solution)/shard_map/ppermute | solution.py:21
  136.8 5.7 %collective-permute-done.28 = f32[3,512]{1,0:T(4,128)S(1)} collective-permute-done((f32[3,512]{1,0:T(4,128)S(1)}, f32[3,512]{1,0:T(4,128)S(1)}, u32[]{:S(2)}, u32[]{:S(2)}) %collective-permute-start.28) | collective-permute-done | bytes 6176 | tf_op jit(solution)/shard_map/ppermute | solution.py:21
  146.1 5.7 %collective-permute-done.30 = f32[3,512]{1,0:T(4,128)S(1)} collective-permute-done((f32[3,512]{1,0:T(4,128)S(1)}, f32[3,512]{1,0:T(4,128)S(1)}, u32[]{:S(2)}, u32[]{:S(2)}) %collective-permute-start.30) | collective-permute-done | bytes 6176 | tf_op jit(solution)/shard_map/ppermute | solution.py:21
  155.4 5.7 %collective-permute-done.32 = f32[3,512]{1,0:T(4,128)S(1)} collective-permute-done((f32[3,512]{1,0:T(4,128)S(1)}, f32[3,512]{1,0:T(4,128)S(1)}, u32[]{:S(2)}, u32[]{:S(2)}) %collective-permute-start.32) | collective-permute-done | bytes 6176 | tf_op jit(solution)/shard_map/ppermute | solution.py:21
  172.9 25.3 %all-gather.5 = f32[256,512]{1,0:T(8,128)S(1)} all-gather(f32[32,512]{1,0:T(8,128)S(1)} %pad_maximum_fusion.6), channel_id=7, replica_groups=mesh['tm_0'=2,'tm_1'=8,'tm_2'=8,'tm_3'=2,'space'=2] {'tm_2'}, dimensions={0}, use_global_device_ids=true | all-gather | bytes 589824 | tf_op jit(solution)/shard_map/all_gather | solution.py:47
  198.3 25.2 %all-gather.6 = f32[256,512]{1,0:T(8,128)S(1)} all-gather(f32[32,512]{1,0:T(8,128)S(1)} %pad_maximum_fusion.7), channel_id=8, replica_groups=mesh['tm_0'=2,'tm_1'=8,'tm_2'=8,'tm_3'=2,'space'=2] {'tm_1'}, dimensions={0}, use_global_device_ids=true | all-gather | bytes 589824 | tf_op jit(solution)/shard_map/all_gather | solution.py:47
  225.5 25.3 %all-gather.1 = f32[256,512]{1,0:T(8,128)S(1)} all-gather(f32[32,512]{1,0:T(8,128)S(1)} %pad_maximum_fusion.3), channel_id=3, replica_groups=mesh['tm_0'=2,'tm_1'=8,'tm_2'=8,'tm_3'=2,'space'=2] {'tm_2'}, dimensions={0}, use_global_device_ids=true | all-gather | bytes 589824 | tf_op jit(solution)/shard_map/all_gather | solution.py:47
  251.0 25.2 %all-gather.2 = f32[256,512]{1,0:T(8,128)S(1)} all-gather(f32[32,512]{1,0:T(8,128)S(1)} %pad_maximum_fusion.4), channel_id=4, replica_groups=mesh['tm_0'=2,'tm_1'=8,'tm_2'=8,'tm_3'=2,'space'=2] {'tm_1'}, dimensions={0}, use_global_device_ids=true | all-gather | bytes 589824 | tf_op jit(solution)/shard_map/all_gather | solution.py:47
  301.2 6.0 %collective-permute-start.41 = (f32[3,512]{1,0:T(4,128)S(1)}, f32[3,512]{1,0:T(4,128)S(1)}, u32[]{:S(2)}, u32[]{:S(2)}) collective-permute-start(f32[3,512]{1,0:T(4,128)S(1)} %get-tuple-element.544), channel_id=1, source_target_pairs={{1,0},{3,2},{5,4},{7,6},{9,8},{11,10},{13,12},{15,14},{17,16},{19,... | collective-permute-start | bytes 18440 | tf_op jit(solution)/shard_map/ppermute | solution.py:22
  308.6 5.7 %collective-permute-done.40 = f32[3,512]{1,0:T(4,128)S(1)} collective-permute-done((f32[3,512]{1,0:T(4,128)S(1)}, f32[3,512]{1,0:T(4,128)S(1)}, u32[]{:S(2)}, u32[]{:S(2)}) %collective-permute-start.40) | collective-permute-done | bytes 6176 | tf_op jit(solution)/shard_map/ppermute | solution.py:21
  327.2 5.7 %collective-permute-done.44 = f32[3,512]{1,0:T(4,128)S(1)} collective-permute-done((f32[3,512]{1,0:T(4,128)S(1)}, f32[3,512]{1,0:T(4,128)S(1)}, u32[]{:S(2)}, u32[]{:S(2)}) %collective-permute-start.44) | collective-permute-done | bytes 6176 | tf_op jit(solution)/shard_map/ppermute | solution.py:21
  336.4 5.7 %collective-permute-done.46 = f32[3,512]{1,0:T(4,128)S(1)} collective-permute-done((f32[3,512]{1,0:T(4,128)S(1)}, f32[3,512]{1,0:T(4,128)S(1)}, u32[]{:S(2)}, u32[]{:S(2)}) %collective-permute-start.46) | collective-permute-done | bytes 6176 | tf_op jit(solution)/shard_map/ppermute | solution.py:21
  355.1 5.7 %collective-permute-done.50 = f32[3,512]{1,0:T(4,128)S(1)} collective-permute-done((f32[3,512]{1,0:T(4,128)S(1)}, f32[3,512]{1,0:T(4,128)S(1)}, u32[]{:S(2)}, u32[]{:S(2)}) %collective-permute-start.50) | collective-permute-done | bytes 6176 | tf_op jit(solution)/shard_map/ppermute | solution.py:21
  364.3 5.7 %collective-permute-done.52 = f32[3,512]{1,0:T(4,128)S(1)} collective-permute-done((f32[3,512]{1,0:T(4,128)S(1)}, f32[3,512]{1,0:T(4,128)S(1)}, u32[]{:S(2)}, u32[]{:S(2)}) %collective-permute-start.52) | collective-permute-done | bytes 6176 | tf_op jit(solution)/shard_map/ppermute | solution.py:21
  373.6 5.7 %collective-permute-done.54 = f32[3,512]{1,0:T(4,128)S(1)} collective-permute-done((f32[3,512]{1,0:T(4,128)S(1)}, f32[3,512]{1,0:T(4,128)S(1)}, u32[]{:S(2)}, u32[]{:S(2)}) %collective-permute-start.54) | collective-permute-done | bytes 6176 | tf_op jit(solution)/shard_map/ppermute | solution.py:21
  383.1 5.7 %collective-permute-done.56 = f32[3,512]{1,0:T(4,128)S(1)} collective-permute-done((f32[3,512]{1,0:T(4,128)S(1)}, f32[3,512]{1,0:T(4,128)S(1)}, u32[]{:S(2)}, u32[]{:S(2)}) %collective-permute-start.56) | collective-permute-done | bytes 6176 | tf_op jit(solution)/shard_map/ppermute | solution.py:21
  392.4 5.7 %collective-permute-done.58 = f32[3,512]{1,0:T(4,128)S(1)} collective-permute-done((f32[3,512]{1,0:T(4,128)S(1)}, f32[3,512]{1,0:T(4,128)S(1)}, u32[]{:S(2)}, u32[]{:S(2)}) %collective-permute-start.58) | collective-permute-done | bytes 6176 | tf_op jit(solution)/shard_map/ppermute | solution.py:21
  401.7 5.7 %collective-permute-done.60 = f32[3,512]{1,0:T(4,128)S(1)} collective-permute-done((f32[3,512]{1,0:T(4,128)S(1)}, f32[3,512]{1,0:T(4,128)S(1)}, u32[]{:S(2)}, u32[]{:S(2)}) %collective-permute-start.60) | collective-permute-done | bytes 6176 | tf_op jit(solution)/shard_map/ppermute | solution.py:21
  411.0 5.7 %collective-permute-done.62 = f32[3,512]{1,0:T(4,128)S(1)} collective-permute-done((f32[3,512]{1,0:T(4,128)S(1)}, f32[3,512]{1,0:T(4,128)S(1)}, u32[]{:S(2)}, u32[]{:S(2)}) %collective-permute-start.62) | collective-permute-done | bytes 6176 | tf_op jit(solution)/shard_map/ppermute | solution.py:21
  420.3 5.7 %collective-permute-done.64 = f32[3,512]{1,0:T(4,128)S(1)} collective-permute-done((f32[3,512]{1,0:T(4,128)S(1)}, f32[3,512]{1,0:T(4,128)S(1)}, u32[]{:S(2)}, u32[]{:S(2)}) %collective-permute-start.64) | collective-permute-done | bytes 6176 | tf_op jit(solution)/shard_map/ppermute | solution.py:21
  426.6 6.9 %psum.28 = f32[16,512]{1,0:T(8,128)S(1)} all-reduce(f32[16,512]{1,0:T(8,128)S(1)} %fusion.4), channel_id=1, replica_groups=mesh['tm_0'=2,'tm_1'=8,'tm_2'=8,'tm_3'=2,'space'=2] {'tm_0'}, use_global_device_ids=true, to_apply=%region_0.1 | all-reduce | flops 8192 | bytes 65536 | tf_op jit(solution)/shard_map/psum | solution.py:72
  433.5 27.1 %psum.29 = f32[16,512]{1,0:T(8,128)S(1)} all-reduce(f32[16,512]{1,0:T(8,128)S(1)} %psum.28), channel_id=1, replica_groups=mesh['tm_0'=2,'tm_1'=8,'tm_2'=8,'tm_3'=2,'space'=2] {'tm_1'}, use_global_device_ids=true, to_apply=%region_1.2 | all-reduce | flops 8192 | bytes 65536 | tf_op jit(solution)/shard_map/psum | solution.py:72
  460.6 27.1 %psum.30 = f32[16,512]{1,0:T(8,128)S(1)} all-reduce(f32[16,512]{1,0:T(8,128)S(1)} %psum.29), channel_id=1, replica_groups=mesh['tm_0'=2,'tm_1'=8,'tm_2'=8,'tm_3'=2,'space'=2] {'tm_2'}, use_global_device_ids=true, to_apply=%region_2.3 | all-reduce | flops 8192 | bytes 65536 | tf_op jit(solution)/shard_map/psum | solution.py:72
  (485 shorter events, 175.6 us)
Async XLA Ops:
  1.5 19.0 %collective-permute-start.4 = (f32[2,3,512]{2,1,0:T(4,128)S(1)}, f32[2,3,512]{2,1,0:T(4,128)S(1)}, u32[]{:S(2)}, u32[]{:S(2)}) collective-permute-start(f32[2,3,512]{2,1,0:T(4,128)S(1)} %get-tuple-element.125), channel_id=1, source_target_pairs={{1,0},{3,2},{5,4},{7,6},{9,8},{11,10},{13,12},{15,14},{17,16},{19,... | collective-permute-start | bytes 36872 | tf_op jit(solution)/shard_map/ppermute | solution.py:22
  4.8 15.7 %collective-permute-start.3 = (f32[2,3,512]{2,1,0:T(4,128)S(1)}, f32[2,3,512]{2,1,0:T(4,128)S(1)}, u32[]{:S(2)}, u32[]{:S(2)}) collective-permute-start(f32[2,3,512]{2,1,0:T(4,128)S(1)} %get-tuple-element.124), channel_id=1, source_target_pairs={{0,1},{2,3},{4,5},{6,7},{8,9},{10,11},{12,13},{14,15},{16,17},{18,... | collective-permute-start | bytes 36872 | tf_op jit(solution)/shard_map/ppermute | solution.py:21
  6.1 14.4 %collective-permute-start.19 = (f32[16,512]{1,0:T(8,128)S(1)}, f32[16,512]{1,0:T(8,128)S(1)}, u32[]{:S(2)}, u32[]{:S(2)}) collective-permute-start(f32[16,512]{1,0:T(8,128)S(1)} %bitcast.959), channel_id=1, source_target_pairs={{2,0},{4,2},{6,4},{8,6},{10,8},{12,10},{14,12},{16,14},{18,16},{20... | collective-permute-start | bytes 98312 | tf_op jit(solution)/shard_map/ppermute | solution.py:30
  18.5 10.5 %collective-permute-start = (f32[16,512]{1,0:T(8,128)S(1)}, f32[16,512]{1,0:T(8,128)S(1)}, u32[]{:S(2)}, u32[]{:S(2)}) collective-permute-start(f32[16,512]{1,0:T(8,128)S(1)} %bitcast.958), channel_id=1, source_target_pairs={{0,2},{2,4},{4,6},{6,8},{8,10},{10,12},{12,14},{14,16},{16,18},{18... | collective-permute-start | bytes 98312 | tf_op jit(solution)/shard_map/ppermute | solution.py:30
  21.3 15.1 %collective-permute-start.21 = (f32[3,512]{1,0:T(4,128)S(1)}, f32[3,512]{1,0:T(4,128)S(1)}, u32[]{:S(2)}, u32[]{:S(2)}) collective-permute-start(f32[3,512]{1,0:T(4,128)S(1)} %get-tuple-element.578), channel_id=1, source_target_pairs={{1,0},{3,2},{5,4},{7,6},{9,8},{11,10},{13,12},{15,14},{17,16},{19,... | collective-permute-start | bytes 18440 | tf_op jit(solution)/shard_map/ppermute | solution.py:22
  27.7 8.7 %collective-permute-start.20 = (f32[3,512]{1,0:T(4,128)S(1)}, f32[3,512]{1,0:T(4,128)S(1)}, u32[]{:S(2)}, u32[]{:S(2)}) collective-permute-start(f32[3,512]{1,0:T(4,128)S(1)} %get-tuple-element.577), channel_id=1, source_target_pairs={{0,1},{2,3},{4,5},{6,7},{8,9},{10,11},{12,13},{14,15},{16,17},{18,... | collective-permute-start | bytes 18440 | tf_op jit(solution)/shard_map/ppermute | solution.py:21
  29.0 7.5 %collective-permute-start.2 = (f32[3,512]{1,0:T(4,128)S(1)}, f32[3,512]{1,0:T(4,128)S(1)}, u32[]{:S(2)}, u32[]{:S(2)}) collective-permute-start(f32[3,512]{1,0:T(4,128)S(1)} %get-tuple-element.576), channel_id=1, source_target_pairs={{1,0},{3,2},{5,4},{7,6},{9,8},{11,10},{13,12},{15,14},{17,16},{19,... | collective-permute-start | bytes 18440 | tf_op jit(solution)/shard_map/ppermute | solution.py:22
  35.1 7.0 %collective-permute-start.1 = (f32[3,512]{1,0:T(4,128)S(1)}, f32[3,512]{1,0:T(4,128)S(1)}, u32[]{:S(2)}, u32[]{:S(2)}) collective-permute-start(f32[3,512]{1,0:T(4,128)S(1)} %get-tuple-element.575), channel_id=1, source_target_pairs={{0,1},{2,3},{4,5},{6,7},{8,9},{10,11},{12,13},{14,15},{16,17},{18,... | collective-permute-start | bytes 18440 | tf_op jit(solution)/shard_map/ppermute | solution.py:21
  44.4 7.0 %collective-permute-start.5 = (f32[3,512]{1,0:T(4,128)S(1)}, f32[3,512]{1,0:T(4,128)S(1)}, u32[]{:S(2)}, u32[]{:S(2)}) collective-permute-start(f32[3,512]{1,0:T(4,128)S(1)} %get-tuple-element.573), channel_id=1, source_target_pairs={{0,1},{2,3},{4,5},{6,7},{8,9},{10,11},{12,13},{14,15},{16,17},{18,... | collective-permute-start | bytes 18440 | tf_op jit(solution)/shard_map/ppermute | solution.py:21
  53.7 7.0 %collective-permute-start.7 = (f32[3,512]{1,0:T(4,128)S(1)}, f32[3,512]{1,0:T(4,128)S(1)}, u32[]{:S(2)}, u32[]{:S(2)}) collective-permute-start(f32[3,512]{1,0:T(4,128)S(1)} %get-tuple-element.571), channel_id=1, source_target_pairs={{0,1},{2,3},{4,5},{6,7},{8,9},{10,11},{12,13},{14,15},{16,17},{18,... | collective-permute-start | bytes 18440 | tf_op jit(solution)/shard_map/ppermute | solution.py:21
  63.0 7.0 %collective-permute-start.9 = (f32[3,512]{1,0:T(4,128)S(1)}, f32[3,512]{1,0:T(4,128)S(1)}, u32[]{:S(2)}, u32[]{:S(2)}) collective-permute-start(f32[3,512]{1,0:T(4,128)S(1)} %get-tuple-element.569), channel_id=1, source_target_pairs={{0,1},{2,3},{4,5},{6,7},{8,9},{10,11},{12,13},{14,15},{16,17},{18,... | collective-permute-start | bytes 18440 | tf_op jit(solution)/shard_map/ppermute | solution.py:21
  72.3 7.0 %collective-permute-start.11 = (f32[3,512]{1,0:T(4,128)S(1)}, f32[3,512]{1,0:T(4,128)S(1)}, u32[]{:S(2)}, u32[]{:S(2)}) collective-permute-start(f32[3,512]{1,0:T(4,128)S(1)} %get-tuple-element.567), channel_id=1, source_target_pairs={{0,1},{2,3},{4,5},{6,7},{8,9},{10,11},{12,13},{14,15},{16,17},{18,... | collective-permute-start | bytes 18440 | tf_op jit(solution)/shard_map/ppermute | solution.py:21
  81.6 7.0 %collective-permute-start.13 = (f32[3,512]{1,0:T(4,128)S(1)}, f32[3,512]{1,0:T(4,128)S(1)}, u32[]{:S(2)}, u32[]{:S(2)}) collective-permute-start(f32[3,512]{1,0:T(4,128)S(1)} %get-tuple-element.565), channel_id=1, source_target_pairs={{0,1},{2,3},{4,5},{6,7},{8,9},{10,11},{12,13},{14,15},{16,17},{18,... | collective-permute-start | bytes 18440 | tf_op jit(solution)/shard_map/ppermute | solution.py:21
  90.9 7.0 %collective-permute-start.15 = (f32[3,512]{1,0:T(4,128)S(1)}, f32[3,512]{1,0:T(4,128)S(1)}, u32[]{:S(2)}, u32[]{:S(2)}) collective-permute-start(f32[3,512]{1,0:T(4,128)S(1)} %get-tuple-element.563), channel_id=1, source_target_pairs={{0,1},{2,3},{4,5},{6,7},{8,9},{10,11},{12,13},{14,15},{16,17},{18,... | collective-permute-start | bytes 18440 | tf_op jit(solution)/shard_map/ppermute | solution.py:21
  98.5 10.3 %collective-permute-start.18 = (f32[3,512]{1,0:T(4,128)S(1)}, f32[3,512]{1,0:T(4,128)S(1)}, u32[]{:S(2)}, u32[]{:S(2)}) collective-permute-start(f32[3,512]{1,0:T(4,128)S(1)} %get-tuple-element.548), channel_id=1, source_target_pairs={{1,0},{3,2},{5,4},{7,6},{9,8},{11,10},{13,12},{15,14},{17,16},{19,... | collective-permute-start | bytes 18440 | tf_op jit(solution)/shard_map/ppermute | solution.py:22
  100.2 8.7 %collective-permute-start.17 = (f32[3,512]{1,0:T(4,128)S(1)}, f32[3,512]{1,0:T(4,128)S(1)}, u32[]{:S(2)}, u32[]{:S(2)}) collective-permute-start(f32[3,512]{1,0:T(4,128)S(1)} %get-tuple-element.547), channel_id=1, source_target_pairs={{0,1},{2,3},{4,5},{6,7},{8,9},{10,11},{12,13},{14,15},{16,17},{18,... | collective-permute-start | bytes 18440 | tf_op jit(solution)/shard_map/ppermute | solution.py:21
  101.5 7.9 %collective-permute-start.23 = (f32[3,512]{1,0:T(4,128)S(1)}, f32[3,512]{1,0:T(4,128)S(1)}, u32[]{:S(2)}, u32[]{:S(2)}) collective-permute-start(f32[3,512]{1,0:T(4,128)S(1)} %get-tuple-element.562), channel_id=1, source_target_pairs={{1,0},{3,2},{5,4},{7,6},{9,8},{11,10},{13,12},{15,14},{17,16},{19,... | collective-permute-start | bytes 18440 | tf_op jit(solution)/shard_map/ppermute | solution.py:22
  107.6 7.0 %collective-permute-start.22 = (f32[3,512]{1,0:T(4,128)S(1)}, f32[3,512]{1,0:T(4,128)S(1)}, u32[]{:S(2)}, u32[]{:S(2)}) collective-permute-start(f32[3,512]{1,0:T(4,128)S(1)} %get-tuple-element.561), channel_id=1, source_target_pairs={{0,1},{2,3},{4,5},{6,7},{8,9},{10,11},{12,13},{14,15},{16,17},{18,... | collective-permute-start | bytes 18440 | tf_op jit(solution)/shard_map/ppermute | solution.py:21
  116.9 7.0 %collective-permute-start.24 = (f32[3,512]{1,0:T(4,128)S(1)}, f32[3,512]{1,0:T(4,128)S(1)}, u32[]{:S(2)}, u32[]{:S(2)}) collective-permute-start(f32[3,512]{1,0:T(4,128)S(1)} %get-tuple-element.559), channel_id=1, source_target_pairs={{0,1},{2,3},{4,5},{6,7},{8,9},{10,11},{12,13},{14,15},{16,17},{18,... | collective-permute-start | bytes 18440 | tf_op jit(solution)/shard_map/ppermute | solution.py:21
  126.2 7.0 %collective-permute-start.26 = (f32[3,512]{1,0:T(4,128)S(1)}, f32[3,512]{1,0:T(4,128)S(1)}, u32[]{:S(2)}, u32[]{:S(2)}) collective-permute-start(f32[3,512]{1,0:T(4,128)S(1)} %get-tuple-element.557), channel_id=1, source_target_pairs={{0,1},{2,3},{4,5},{6,7},{8,9},{10,11},{12,13},{14,15},{16,17},{18,... | collective-permute-start | bytes 18440 | tf_op jit(solution)/shard_map/ppermute | solution.py:21
  154.0 7.0 %collective-permute-start.32 = (f32[3,512]{1,0:T(4,128)S(1)}, f32[3,512]{1,0:T(4,128)S(1)}, u32[]{:S(2)}, u32[]{:S(2)}) collective-permute-start(f32[3,512]{1,0:T(4,128)S(1)} %get-tuple-element.551), channel_id=1, source_target_pairs={{0,1},{2,3},{4,5},{6,7},{8,9},{10,11},{12,13},{14,15},{16,17},{18,... | collective-permute-start | bytes 18440 | tf_op jit(solution)/shard_map/ppermute | solution.py:21
  163.3 7.0 %collective-permute-start.34 = (f32[3,512]{1,0:T(4,128)S(1)}, f32[3,512]{1,0:T(4,128)S(1)}, u32[]{:S(2)}, u32[]{:S(2)}) collective-permute-start(f32[3,512]{1,0:T(4,128)S(1)} %get-tuple-element.549), channel_id=1, source_target_pairs={{0,1},{2,3},{4,5},{6,7},{8,9},{10,11},{12,13},{14,15},{16,17},{18,... | collective-permute-start | bytes 18440 | tf_op jit(solution)/shard_map/ppermute | solution.py:21
  281.4 7.1 %collective-permute-start.36 = (f32[16,512]{1,0:T(8,128)S(1)}, f32[16,512]{1,0:T(8,128)S(1)}, u32[]{:S(2)}, u32[]{:S(2)}) collective-permute-start(f32[16,512]{1,0:T(8,128)S(1)} %fusion.55), channel_id=1, source_target_pairs={{2,0},{4,2},{6,4},{8,6},{10,8},{12,10},{14,12},{16,14},{18,16},{20... | collective-permute-start | bytes 98312 | tf_op jit(solution)/shard_map/ppermute | solution.py:30
  290.4 7.0 %collective-permute-start.37 = (f32[3,512]{1,0:T(4,128)S(1)}, f32[3,512]{1,0:T(4,128)S(1)}, u32[]{:S(2)}, u32[]{:S(2)}) collective-permute-start(f32[3,512]{1,0:T(4,128)S(1)} %get-tuple-element.529), channel_id=1, source_target_pairs={{0,1},{2,3},{4,5},{6,7},{8,9},{10,11},{12,13},{14,15},{16,17},{18,... | collective-permute-start | bytes 18440 | tf_op jit(solution)/shard_map/ppermute | solution.py:21
  291.7 9.5 %collective-permute-start.39 = (f32[16,512]{1,0:T(8,128)S(1)}, f32[16,512]{1,0:T(8,128)S(1)}, u32[]{:S(2)}, u32[]{:S(2)}) collective-permute-start(f32[16,512]{1,0:T(8,128)S(1)} %get-tuple-element.54), channel_id=1, source_target_pairs={{0,2},{2,4},{4,6},{6,8},{8,10},{10,12},{12,14},{14,16},{16,18},{18... | collective-permute-start | bytes 98312 | tf_op jit(solution)/shard_map/ppermute | solution.py:30
  301.2 7.4 %collective-permute-start.41 = (f32[3,512]{1,0:T(4,128)S(1)}, f32[3,512]{1,0:T(4,128)S(1)}, u32[]{:S(2)}, u32[]{:S(2)}) collective-permute-start(f32[3,512]{1,0:T(4,128)S(1)} %get-tuple-element.544), channel_id=1, source_target_pairs={{1,0},{3,2},{5,4},{7,6},{9,8},{11,10},{13,12},{15,14},{17,16},{19,... | collective-permute-start | bytes 18440 | tf_op jit(solution)/shard_map/ppermute | solution.py:22
  316.5 7.0 %collective-permute-start.42 = (f32[3,512]{1,0:T(4,128)S(1)}, f32[3,512]{1,0:T(4,128)S(1)}, u32[]{:S(2)}, u32[]{:S(2)}) collective-permute-start(f32[3,512]{1,0:T(4,128)S(1)} %get-tuple-element.541), channel_id=1, source_target_pairs={{0,1},{2,3},{4,5},{6,7},{8,9},{10,11},{12,13},{14,15},{16,17},{18,... | collective-permute-start | bytes 18440 | tf_op jit(solution)/shard_map/ppermute | solution.py:21
  325.8 7.0 %collective-permute-start.44 = (f32[3,512]{1,0:T(4,128)S(1)}, f32[3,512]{1,0:T(4,128)S(1)}, u32[]{:S(2)}, u32[]{:S(2)}) collective-permute-start(f32[3,512]{1,0:T(4,128)S(1)} %get-tuple-element.539), channel_id=1, source_target_pairs={{0,1},{2,3},{4,5},{6,7},{8,9},{10,11},{12,13},{14,15},{16,17},{18,... | collective-permute-start | bytes 18440 | tf_op jit(solution)/shard_map/ppermute | solution.py:21
  363.0 7.0 %collective-permute-start.52 = (f32[3,512]{1,0:T(4,128)S(1)}, f32[3,512]{1,0:T(4,128)S(1)}, u32[]{:S(2)}, u32[]{:S(2)}) collective-permute-start(f32[3,512]{1,0:T(4,128)S(1)} %get-tuple-element.531), channel_id=1, source_target_pairs={{0,1},{2,3},{4,5},{6,7},{8,9},{10,11},{12,13},{14,15},{16,17},{18,... | collective-permute-start | bytes 18440 | tf_op jit(solution)/shard_map/ppermute | solution.py:21
  372.3 7.0 %collective-permute-start.54 = (f32[3,512]{1,0:T(4,128)S(1)}, f32[3,512]{1,0:T(4,128)S(1)}, u32[]{:S(2)}, u32[]{:S(2)}) collective-permute-start(f32[3,512]{1,0:T(4,128)S(1)} %get-tuple-element.527), channel_id=1, source_target_pairs={{0,1},{2,3},{4,5},{6,7},{8,9},{10,11},{12,13},{14,15},{16,17},{18,... | collective-permute-start | bytes 18440 | tf_op jit(solution)/shard_map/ppermute | solution.py:21
  381.6 7.2 %collective-permute-start.56 = (f32[3,512]{1,0:T(4,128)S(1)}, f32[3,512]{1,0:T(4,128)S(1)}, u32[]{:S(2)}, u32[]{:S(2)}) collective-permute-start(f32[3,512]{1,0:T(4,128)S(1)} %get-tuple-element.525), channel_id=1, source_target_pairs={{0,1},{2,3},{4,5},{6,7},{8,9},{10,11},{12,13},{14,15},{16,17},{18,... | collective-permute-start | bytes 18440 | tf_op jit(solution)/shard_map/ppermute | solution.py:21
  391.1 7.0 %collective-permute-start.58 = (f32[3,512]{1,0:T(4,128)S(1)}, f32[3,512]{1,0:T(4,128)S(1)}, u32[]{:S(2)}, u32[]{:S(2)}) collective-permute-start(f32[3,512]{1,0:T(4,128)S(1)} %get-tuple-element.523), channel_id=1, source_target_pairs={{0,1},{2,3},{4,5},{6,7},{8,9},{10,11},{12,13},{14,15},{16,17},{18,... | collective-permute-start | bytes 18440 | tf_op jit(solution)/shard_map/ppermute | solution.py:21
  (43 other events, 373.0 us)
where the time goes:
time: 495 us; the launch traced here: 492 us
  blocking collectives  180 us (36%)
  waiting for transfers between devices  161 us (33%)
  starting transfers between devices  129 us (26%)
  other arithmetic  10.3 us (2%)
  local copies, waits for them, and re-layouts  8.67 us (2%)
    ppermute x31, waiting for transfers between devices, with_halo(): before = lax.ppermute(last, axis, up)  157 us
    all_gather x8, blocking collectives, all_in_one(): both, at, found = (lax.all_gather(jnp.concatenate(lines), axis), 0, {})  115 us
    ppermute x31, starting transfers between devices, with_halo(): after = lax.ppermute(leading, axis, down)  70.6 us
    psum x4, blocking collectives, by_axis(): return functools.reduce(lax.psum, axes, value)  64.4 us
    ppermute x31, starting transfers between devices, with_halo(): before = lax.ppermute(last, axis, up)  40.2 us
    ppermute x4, starting transfers between devices, passed_along(): return lax.ppermute(block, axis, route)  18.1 us
  transfers between devices with their start and end apart: 66, of which 29 were waited for; matrix products, arithmetic and copies ran while one was open for 0% of the time, Pallas kernels for 0%

commit v1 on v0

v1 whole, which is shorter than its diff:
```python
import jax
import jax.numpy as jnp
from jax import lax
from jax.experimental import pallas as pl
from jax.experimental.pallas import tpu as pltpu
from jax.sharding import Mesh
from jax.sharding import PartitionSpec as P

SWEEPS = 3
COARSEN = 8
SLABS = 256
TM = ("tm_0", "tm_1", "tm_2", "tm_3")
ROWS = 16
COLS = 512
LANES = 128
TILES = COLS // LANES
PHASES = 4

ENTRY, FORWARD, ADJOINT, TARGET, CONTROL, SPREAD, REACTION = range(7)
WEIGHT, INVERSE, DAMPING, ALPHA, BETA, GAMMA, SOURCE, STATE, TOTAL, FW_LESS, AD_LESS = range(11)


def tm_index():
    return ((lax.axis_index("tm_0") * 8 + lax.axis_index("tm_1")) * 8 + lax.axis_index("tm_2")) * 2 + lax.axis_index(
        "tm_3"
    )


def each(fn, *fields):
    return [[fn(*(f[p][t] for f in fields)) for t in range(TILES)] for p in range(PHASES)]


def load(ref, *at):
    return [[ref[(*at, p, slice(None), pl.ds(t * LANES, LANES))] for t in range(TILES)] for p in range(PHASES)]


def store(value, ref, *at):
    for p in range(PHASES):
        for t in range(TILES):
            ref[(*at, p, slice(None), pl.ds(t * LANES, LANES))] = value[p][t]


def make_neighbours(space):
    sub = lax.broadcasted_iota(jnp.int32, (8, LANES), 0)
    lane = lax.broadcasted_iota(jnp.int32, (8, LANES), 1)
    up_ok = sub != 4 * space
    down_ok = sub != 7 - 4 * space
    first, last = (lane == 0, lane == LANES - 1)

    def neighbours(v):
        above = [jnp.where(up_ok, pltpu.roll(v[PHASES - 1][t], 1, 0), 0.0) for t in range(TILES)]
        below = [jnp.where(down_ok, pltpu.roll(v[0][t], 7, 0), 0.0) for t in range(TILES)]
        out = []
        for p in range(PHASES):
            ups = v[p - 1] if p else above
            downs = v[p + 1] if p < PHASES - 1 else below
            right = [pltpu.roll(v[p][t], 1, 1) for t in range(TILES)]
            left = [pltpu.roll(v[p][t], LANES - 1, 1) for t in range(TILES)]
            row = []
            for t in range(TILES):
                a = jnp.where(first, right[t - 1] if t else 0.0, right[t])
                b = jnp.where(last, left[t + 1] if t < TILES - 1 else 0.0, left[t])
                row.append((ups[t] + downs[t]) + (a + b))
            out.append(row)
        return out

    return neighbours


def relax_kernel(own_ref, other_ref, chan_ref, keep_ref, raw, grid, field, points, coarse_points):
    slab = tm_index()
    space = lax.axis_index("space")
    neighbours = make_neighbours(space)
    is_last = slab == SLABS - 1
    not_last = jnp.where(is_last, 0.0, 1.0)
    not_first = jnp.where(slab == 0, 0.0, 1.0)

    for n in range(7):
        for t in range(TILES):
            cols = pl.ds(t * LANES, LANES)
            raw[n, t, 0:ROWS, :] = own_ref[n, :, cols]
            raw[n, t, ROWS : 2 * ROWS, :] = other_ref[n, :, cols]
    for n in range(7):
        for p in range(PHASES):
            for t in range(TILES):
                grid[n, p, :, pl.ds(t * LANES, LANES)] = raw[n, t, pl.ds(p, 8, stride=PHASES), :]

    spread, reaction = (load(grid, SPREAD), load(grid, REACTION))
    inverse = each(lambda s, r: 1.0 / (1.0 + 4.0 * s + r), spread, reaction)
    store(inverse, field, INVERSE)
    store(each(lambda s, i: s * i, spread, inverse), field, WEIGHT)
    store(each(lambda r: 1.0 / (1.0 + COARSEN * r), reaction), field, DAMPING)

    def forward_step(right_side):
        weight, scaled = (load(field, WEIGHT), each(lambda r, i: r * i, right_side, load(field, INVERSE)))
        v = right_side
        for _ in range(SWEEPS):
            v = each(lambda s, w, n: s + w * n, scaled, weight, neighbours(v))
        return v

    def adjoint_step(y):
        weight = load(field, WEIGHT)
        carried, summed = (y, y)
        for _ in range(SWEEPS - 1):
            carried = neighbours(each(jnp.multiply, weight, carried))
            summed = each(jnp.add, summed, carried)
        final = neighbours(each(jnp.multiply, weight, carried))
        return each(lambda s, i, f: s * i + f, summed, load(field, INVERSE), final)

    store(load(grid, ENTRY), field, STATE)

    def forward_body(i, _):
        v = forward_step(each(jnp.add, load(field, STATE), load(grid, CONTROL)))
        store(v, field, STATE)
        store(v, points, i)
        return 0

    lax.fori_loop(0, COARSEN, forward_body, 0)

    damping = load(field, DAMPING)
    forward_less = jnp.where(is_last, SLABS - 1, SLABS - 2 - slab)
    adjoint_less = jnp.maximum(slab - 1, 0)
    for slot, count in ((FW_LESS, forward_less), (AD_LESS, adjoint_less)):
        power, block = (damping, each(jnp.ones_like, damping))
        total = each(jnp.zeros_like, damping)
        for b in range(8):
            taken = ((count >> b) & 1) == 1
            total = each(lambda s, v, q: jnp.where(taken, v + q * s, s), total, block, power)
            if b < 7:
                block = each(lambda v, q: v + v * q, block, power)
                power = each(lambda q: q * q, power)
        store(total, field, slot)

    push = each(
        lambda f, d, g: f - not_last * (d * g), load(field, STATE), damping, load(grid, FORWARD)
    )
    store(push, field, SOURCE)
    store(
        each(lambda w, u, e: w * u + (1.0 - not_last) * e, load(field, FW_LESS), push, load(grid, ENTRY)),
        field,
        STATE,
    )
    store(each(jnp.zeros_like, damping), field, ALPHA)
    store(load(grid, ADJOINT), field, BETA)
    store(each(lambda g: g / COARSEN, load(grid, FORWARD)), field, GAMMA)

    def adjoint_body(n, _):
        at = COARSEN - 1 - n
        share = jnp.where(n == 0, 0.0, 1.0 / COARSEN)
        store(adjoint_step(each(lambda a, f: a + share * f, load(field, ALPHA), load(points, at))), field, ALPHA)
        store(adjoint_step(load(field, BETA)), field, BETA)
        store(
            adjoint_step(each(lambda a, o: a - o / COARSEN, load(field, GAMMA), load(grid, TARGET))), field, GAMMA
        )
        v = forward_step(each(jnp.add, load(field, STATE), load(grid, CONTROL)))
        store(v, field, STATE)
        store(v, coarse_points, n)
        return 0

    lax.fori_loop(0, COARSEN, adjoint_body, 0)

    damping = load(field, DAMPING)
    alpha, beta, gamma = (load(field, ALPHA), load(field, BETA), load(field, GAMMA))
    keep = each(lambda g, d, a: g + not_last * (d * a), gamma, damping, alpha)
    pull = each(
        lambda k, d, g, b: d * (k - g) + b, keep, damping, load(grid, ADJOINT), beta
    )
    push = load(field, SOURCE)
    less = load(field, AD_LESS)
    store(
        each(lambda a, k, w, q, d: a + k + not_first * ((1.0 + d * w) * q), alpha, keep, less, pull, damping),
        field,
        TOTAL,
    )
    rest = each(lambda a, k, w, q: not_last * a + not_first * (k + w * q), alpha, keep, less, pull)
    store(
        each(
            lambda t, w, d, u, o: t + ((1.0 + d * w) * u - o) / COARSEN,
            rest,
            load(field, FW_LESS),
            damping,
            push,
            load(grid, TARGET),
        ),
        field,
        GAMMA,
    )
    store(pull, field, BETA)
    store(keep, field, STATE)

    def gradient_body(n, _):
        v = adjoint_step(load(field, GAMMA))
        store(each(jnp.add, load(field, TOTAL), v), field, TOTAL)
        at = COARSEN - 2 - n
        store(
            each(lambda a, f, o: a + (f - o) / COARSEN, v, load(coarse_points, at), load(grid, TARGET)), field, GAMMA
        )
        return 0

    lax.fori_loop(0, COARSEN - 1, gradient_body, 0)

    for n, slot in enumerate((SOURCE, BETA, ALPHA, TOTAL)):
        for p in range(PHASES):
            for t in range(TILES):
                block = field[slot, p, 0:4, pl.ds(t * LANES, LANES)]
                chan_ref[pl.ds((n * TILES + t) * ROWS + p, 4, stride=PHASES), :] = block
    for p in range(PHASES):
        for t in range(TILES):
            keep_ref[pl.ds(t * ROWS + p, 4, stride=PHASES), :] = field[STATE, p, 0:4, pl.ds(t * LANES, LANES)]


def chain_kernel(got_ref, reaction_ref, out_ref):
    owner = tm_index()
    role = owner // 64
    cell = owner % 64
    tile = cell // ROWS
    row = reaction_ref[pl.ds(cell % ROWS, 1), :]
    reaction = row[:, 0:LANES]
    for t in range(1, TILES):
        reaction = jnp.where(tile == t, row[:, t * LANES : (t + 1) * LANES], reaction)
    d = jnp.broadcast_to(1.0 / (1.0 + COARSEN * reaction), (8, LANES))
    length = SLABS // 8
    sub = lax.broadcasted_iota(jnp.int32, (8, LANES), 0)
    d32 = d
    for _ in range(5):
        d32 = d32 * d32
    d64 = d32 * d32
    d128 = d64 * d64

    def strided(i):
        return pl.ds(i, 8, stride=length)

    @pl.when(role == 0)
    def _():
        x = pltpu.roll(got_ref[strided(length - 1), :], 1, 0)
        local = [x]
        for i in range(1, length):
            x = d * x + got_ref[strided(i - 1), :]
            local.append(x)
        c = x
        c = c + jnp.where(sub >= 1, d32 * pltpu.roll(c, 1, 0), 0.0)
        c = c + jnp.where(sub >= 2, d64 * pltpu.roll(c, 2, 0), 0.0)
        c = c + jnp.where(sub >= 4, d128 * pltpu.roll(c, 4, 0), 0.0)
        c = jnp.where(sub >= 1, pltpu.roll(c, 1, 0), 0.0)
        for i in range(length):
            c = d * c
            out_ref[strided(i), :] = local[i] + c

    @pl.when(role == 1)
    def _():
        x = jnp.where(sub == 7, 0.0, pltpu.roll(got_ref[strided(0), :], 7, 0))
        local = [x]
        for i in range(length - 2, -1, -1):
            x = d * x + got_ref[strided(i + 1), :]
            local.append(x)
        c = x
        c = c + jnp.where(sub < 7, d32 * pltpu.roll(c, 7, 0), 0.0)
        c = c + jnp.where(sub < 6, d64 * pltpu.roll(c, 6, 0), 0.0)
        c = c + jnp.where(sub < 4, d128 * pltpu.roll(c, 4, 0), 0.0)
        c = jnp.where(sub < 7, pltpu.roll(c, 7, 0), 0.0)
        for n in range(length):
            c = d * c
            out_ref[strided(length - 1 - n), :] = local[n] + c

    @pl.when(role == 2)
    def _():
        out_ref[strided(0), :] = pltpu.roll(got_ref[strided(length - 1), :], 1, 0)
        for i in range(1, length):
            out_ref[strided(i), :] = got_ref[strided(i - 1), :]

    @pl.when(role == 3)
    def _():
        parts = [got_ref[pl.ds(8 * i, 8), :] for i in range(length)]
        while len(parts) > 1:
            parts = [a + b for a, b in zip(parts[::2], parts[1::2])]
        total = jnp.sum(parts[0], axis=0, keepdims=True) * (1.0 / (COARSEN * SLABS))
        total = jnp.broadcast_to(total, (8, LANES))
        for i in range(length):
            out_ref[pl.ds(8 * i, 8), :] = total


def finish_kernel(got_ref, keep_ref, forward_ref, adjoint_ref, gradient_ref):
    for t in range(TILES):
        cols = pl.ds(t * LANES, LANES)
        forward, scanned, passed, gradient = (got_ref[pl.ds(64 * n + t * ROWS, ROWS), :] for n in range(4))
        forward_ref[:, cols] = forward
        adjoint_ref[:, cols] = scanned + (passed + keep_ref[pl.ds(t * ROWS, ROWS), :])
        gradient_ref[:, cols] = gradient


def in_vmem(count):
    return [pl.BlockSpec(memory_space=pltpu.VMEM)] * count


def field_shape(*lead):
    return pltpu.VMEM((*lead, PHASES, 8, COLS), jnp.float32)


def shards(control, initial, diffusion, reaction, forward_guess, adjoint_guess, observed):
    own_forward = forward_guess[0]
    entry = jnp.where(tm_index() == SLABS - 1, initial, own_forward)
    own = jnp.stack((entry, own_forward, adjoint_guess[0], observed[0], control, diffusion, reaction))
    other = lax.ppermute(own, "space", [(0, 1), (1, 0)])
    block = jax.ShapeDtypeStruct((ROWS, COLS), jnp.float32)
    rows = jax.ShapeDtypeStruct((SLABS, LANES), jnp.float32)
    channels, keep = pl.pallas_call(
        relax_kernel,
        out_shape=(rows, jax.ShapeDtypeStruct((64, LANES), jnp.float32)),
        in_specs=in_vmem(2),
        out_specs=in_vmem(2),
        scratch_shapes=[
            pltpu.VMEM((7, TILES, 2 * ROWS, LANES), jnp.float32),
            field_shape(7),
            field_shape(11),
            field_shape(COARSEN),
            field_shape(COARSEN),
        ],
        name="relax",
    )(own, other)
    got = lax.all_to_all(channels, TM, 0, 0, tiled=True)
    sent = pl.pallas_call(
        chain_kernel, out_shape=rows, in_specs=in_vmem(2), out_specs=in_vmem(1)[0], name="chain"
    )(got, reaction)
    back = lax.all_to_all(sent, TM, 0, 0, tiled=True)
    forward_states, adjoint_states, gradient = pl.pallas_call(
        finish_kernel, out_shape=(block, block, block), in_specs=in_vmem(2), out_specs=in_vmem(3), name="finish"
    )(back, keep)
    return (forward_states[None], adjoint_states[None], gradient)


def solution(mesh):
    finer = Mesh(
        mesh.devices.reshape(2, 8, 8, 2, mesh.shape["space"]),
        ("tm_0", "tm_1", "tm_2", "tm_3", "space"),
    )
    return jax.shard_map(
        shards,
        mesh=finer,
        in_specs=(
            P("space", None),
            P("space", None),
            P("space", None),
            P("space", None),
            P(TM, "space", None),
            P(TM, "space", None),
            P(TM, "space", None),
        ),
        out_specs=(P(TM, "space", None), P(TM, "space", None), P("space", None)),
        check_vma=False,
    )
```

time: 495 us -> 90.7 us (0.18)
  the two profiles are of different devices: /device:TPU:6 before, /device:TPU:1 now
where the time goes in v1:
time: 90.7 us; the launch traced here: 89.9 us
  blocking collectives  59.8 us (66%)
  Pallas kernels  15.4 us (17%)
  starting transfers between devices  5.47 us (6%)
  local copies, waits for them, and re-layouts  5.21 us (6%)
  waiting for transfers between devices  3.4 us (4%)
    all_to_all x1, blocking collectives, shards(): got = lax.all_to_all(channels, TM, 0, 0, tiled=True)  37.1 us
    all_to_all x1, blocking collectives, shards(): back = lax.all_to_all(sent, TM, 0, 0, tiled=True)  22.7 us
    pallas_call x1, Pallas kernels, shards(): pl.pallas_call(relax_kernel, out_shape=(rows, jax.ShapeDtypeStruct((64, L...  12.1 us
    ppermute x1, starting transfers between devices, shards(): other = lax.ppermute(own, 'space', [(0, 1), (1, 0)])  5.47 us
    unnamed x21, local copies, waits for them, and re-layouts  5.2 us
    ppermute x1, waiting for transfers between devices, shards(): other = lax.ppermute(own, 'space', [(0, 1), (1, 0)])  3.4 us
  transfers between devices with their start and end apart: 1, of which 1 were waited for; matrix products, arithmetic and copies ran while one was open for 0% of the time, Pallas kernels for 0%

profile of v1, /device:TPU:1, one launch (start us, length us, event | category | flops | bytes accessed | tf_op | source)
XLA Modules:
  0.0 89.9 jit_solution(2453794416928297375)
XLA Ops:
  0.6 0.0 copy-start.2
  0.7 0.7 copy-done.2
  1.4 0.0 copy-start.4
  1.4 0.7 copy-done.4
  2.2 0.0 copy-start.5
  2.2 0.8 copy-done.5
  2.9 0.0 copy-start.6
  2.9 0.8 copy-done.6
  3.7 0.0 copy-start.7
  3.7 0.8 copy-done.7
  4.4 0.0 copy-start.3
  4.4 0.8 copy-done.3
  5.2 0.0 copy-start
  5.2 5.5 %collective-permute-start = (f32[7,16,512]{2,1,0:T(8,128)S(1)}, f32[7,16,512]{2,1,0:T(8,128)S(1)}, u32[]{:S(2)}, u32[]{:S(2)}) collective-permute-start(f32[7,16,512]{2,1,0:T(8,128)S(1)} %bitcast_dynamic-update-slice_fusion.own_ref), channel_id=1, source_target_pairs={{0,1},{1,0},{2,3},{3,2},{4,5},{5,4},{6,7},{7,6},{8,9},{9,8},{10,11... | collective-permute-start | bytes 688136 | tf_op jit(solution)/shard_map/ppermute | solution.py:303
  10.7 3.4 %collective-permute-done.other_ref = f32[7,16,512]{2,1,0:T(8,128)S(1)} collective-permute-done((f32[7,16,512]{2,1,0:T(8,128)S(1)}, f32[7,16,512]{2,1,0:T(8,128)S(1)}, u32[]{:S(2)}, u32[]{:S(2)}) %collective-permute-start) | collective-permute-done | bytes 229408 | tf_op jit(solution)/shard_map/ppermute | solution.py:303
  14.1 0.0 copy-done
  14.1 0.0 copy-start.1
  14.1 0.7 copy-done.1
  14.8 12.1 %relax.1 = (f32[256,128]{1,0:T(8,128)}, f32[64,128]{1,0:T(8,128)}) custom-call(f32[7,16,512]{2,1,0:T(8,128)} %copy-done, f32[7,16,512]{2,1,0:T(8,128)} %copy-done.1), custom_call_target="tpu_custom_call" | custom-call | tf_op jit(solution)/shard_map/relax/pallas_call | solution.py:306
  26.9 37.1 %all_to_all.22 = f32[256,1,128]{2,1,0:T(1,128)} all-to-all(f32[256,1,128]{2,1,0:T(1,128)} %bitcast.25), channel_id=1, replica_groups=mesh['tm_0'=2,'tm_1'=8,'tm_2'=8,'tm_3'=2,'space'=2] {'tm_0','tm_1','tm_2..., dimensions={0} | all-to-all | bytes 262144 | tf_op jit(solution)/shard_map/all_to_all | solution.py:320
  63.9 1.8 %chain.1 = f32[256,128]{1,0:T(8,128)} custom-call(f32[256,128]{1,0:T(8,128)} %bitcast.23, f32[16,512]{1,0:T(8,128)} %reaction_ref.1), custom_call_target="tpu_custom_call" | custom-call | tf_op jit(solution)/shard_map/chain/pallas_call | solution.py:321
  65.7 22.7 %all_to_all.23 = f32[256,1,128]{2,1,0:T(1,128)} all-to-all(f32[256,1,128]{2,1,0:T(1,128)} %bitcast.24), channel_id=1, replica_groups=mesh['tm_0'=2,'tm_1'=8,'tm_2'=8,'tm_3'=2,'space'=2] {'tm_0','tm_1','tm_2..., dimensions={0} | all-to-all | bytes 262144 | tf_op jit(solution)/shard_map/all_to_all | solution.py:324
  88.4 1.6 %finish.1 = (f32[16,512]{1,0:T(8,128)}, f32[16,512]{1,0:T(8,128)}, f32[16,512]{1,0:T(8,128)}) custom-call(f32[256,128]{1,0:T(8,128)} %bitcast.22, f32[64,128]{1,0:T(8,128)} %get-tuple-element.9.keep_ref), custom_call_target="tpu_custom_call" | custom-call | tf_op jit(solution)/shard_map/finish/pallas_call | solution.py:325
  (7 shorter events, 0.0 us)
Async XLA Ops:
  0.6 0.8 copy-start.2
  1.4 0.8 copy-start.4
  2.2 0.8 copy-start.5
  2.9 0.8 copy-start.6
  3.7 0.8 copy-start.7
  4.4 0.8 copy-start.3
  5.2 8.9 %copy-start = (f32[7,16,512]{2,1,0:T(8,128)}, f32[7,16,512]{2,1,0:T(8,128)S(1)}, u32[]{:S(2)}) copy-start(f32[7,16,512]{2,1,0:T(8,128)S(1)} %bitcast_dynamic-update-slice_fusion.own_ref) | copy-start | bytes 688132
  5.2 8.9 %collective-permute-start = (f32[7,16,512]{2,1,0:T(8,128)S(1)}, f32[7,16,512]{2,1,0:T(8,128)S(1)}, u32[]{:S(2)}, u32[]{:S(2)}) collective-permute-start(f32[7,16,512]{2,1,0:T(8,128)S(1)} %bitcast_dynamic-update-slice_fusion.own_ref), channel_id=1, source_target_pairs={{0,1},{1,0},{2,3},{3,2},{4,5},{5,4},{6,7},{7,6},{8,9},{9,8},{10,11... | collective-permute-start | bytes 688136 | tf_op jit(solution)/shard_map/ppermute | solution.py:303
  14.1 0.7 copy-start.1

commit v2 on v1

--- a/solution.py
+++ b/solution.py
@@ -24,6 +24,10 @@
     return ((lax.axis_index("tm_0") * 8 + lax.axis_index("tm_1")) * 8 + lax.axis_index("tm_2")) * 2 + lax.axis_index(
         "tm_3"
     )
+
+
+def space_index():
+    return lax.axis_index("space")
 
 
 def each(fn, *fields):
@@ -67,9 +71,38 @@
     return neighbours
 
 
+def pack_kernel(control, initial, diffusion, reaction, forward, adjoint, observed, out_ref, sems):
+    is_last = tm_index() == SLABS - 1
+
+    def copy(source, slot):
+        return pltpu.make_async_copy(source, out_ref.at[slot], sems.at[slot])
+
+    @pl.when(is_last)
+    def _():
+        copy(initial, ENTRY).start()
+
+    @pl.when(jnp.logical_not(is_last))
+    def _():
+        copy(forward, ENTRY).start()
+
+    rest = (
+        (forward, FORWARD),
+        (adjoint, ADJOINT),
+        (observed, TARGET),
+        (control, CONTROL),
+        (diffusion, SPREAD),
+        (reaction, REACTION),
+    )
+    for source, slot in rest:
+        copy(source, slot).start()
+    copy(forward, ENTRY).wait()
+    for source, slot in rest:
+        copy(source, slot).wait()
+
+
 def relax_kernel(own_ref, other_ref, chan_ref, keep_ref, raw, grid, field, points, coarse_points):
     slab = tm_index()
-    space = lax.axis_index("space")
+    space = space_index()
     neighbours = make_neighbours(space)
     is_last = slab == SLABS - 1
     not_last = jnp.where(is_last, 0.0, 1.0)
@@ -209,12 +242,12 @@
             keep_ref[pl.ds(t * ROWS + p, 4, stride=PHASES), :] = field[STATE, p, 0:4, pl.ds(t * LANES, LANES)]
 
 
-def chain_kernel(got_ref, reaction_ref, out_ref):
+def chain_kernel(got_ref, own_ref, out_ref):
     owner = tm_index()
     role = owner // 64
     cell = owner % 64
     tile = cell // ROWS
-    row = reaction_ref[pl.ds(cell % ROWS, 1), :]
+    row = own_ref[REACTION, pl.ds(cell % ROWS, 1), :]
     reaction = row[:, 0:LANES]
     for t in range(1, TILES):
         reaction = jnp.where(tile == t, row[:, t * LANES : (t + 1) * LANES], reaction)
@@ -292,20 +325,30 @@
     return [pl.BlockSpec(memory_space=pltpu.VMEM)] * count
 
 
+def in_place(value):
+    return pltpu.with_memory_space_constraint(value, pltpu.VMEM)
+
+
 def field_shape(*lead):
     return pltpu.VMEM((*lead, PHASES, 8, COLS), jnp.float32)
 
 
 def shards(control, initial, diffusion, reaction, forward_guess, adjoint_guess, observed):
-    own_forward = forward_guess[0]
-    entry = jnp.where(tm_index() == SLABS - 1, initial, own_forward)
-    own = jnp.stack((entry, own_forward, adjoint_guess[0], observed[0], control, diffusion, reaction))
+    own = pl.pallas_call(
+        pack_kernel,
+        out_shape=pltpu.VMEM((7, ROWS, COLS), jnp.float32),
+        in_specs=[pl.BlockSpec(memory_space=pl.ANY)] * 7,
+        out_specs=in_vmem(1)[0],
+        scratch_shapes=[pltpu.SemaphoreType.DMA((7,))],
+        name="pack",
+    )(control, initial, diffusion, reaction, forward_guess[0], adjoint_guess[0], observed[0])
     other = lax.ppermute(own, "space", [(0, 1), (1, 0)])
+    own, other = in_place(own), in_place(other)
     block = jax.ShapeDtypeStruct((ROWS, COLS), jnp.float32)
-    rows = jax.ShapeDtypeStruct((SLABS, LANES), jnp.float32)
+    rows = pltpu.VMEM((SLABS, LANES), jnp.float32)
     channels, keep = pl.pallas_call(
         relax_kernel,
-        out_shape=(rows, jax.ShapeDtypeStruct((64, LANES), jnp.float32)),
+        out_shape=(rows, pltpu.VMEM((64, LANES), jnp.float32)),
         in_specs=in_vmem(2),
         out_specs=in_vmem(2),
         scratch_shapes=[
@@ -317,11 +360,12 @@
         ],
         name="relax",
     )(own, other)
-    got = lax.all_to_all(channels, TM, 0, 0, tiled=True)
+    got = in_place(lax.all_to_all(channels, TM, 0, 0, tiled=True))
     sent = pl.pallas_call(
         chain_kernel, out_shape=rows, in_specs=in_vmem(2), out_specs=in_vmem(1)[0], name="chain"
-    )(got, reaction)
-    back = lax.all_to_all(sent, TM, 0, 0, tiled=True)
+    )(got, own)
+    back = in_place(lax.all_to_all(sent, TM, 0, 0, tiled=True))
+    keep = in_place(keep)
     forward_states, adjoint_states, gradient = pl.pallas_call(
         finish_kernel, out_shape=(block, block, block), in_specs=in_vmem(2), out_specs=in_vmem(3), name="finish"
     )(back, keep)

time: 90.7 us -> 79.4 us (0.88)
  local copies, waits for them, and re-layouts: 5.21 us -> 0 us
  Pallas kernels: 15.4 us -> 12.2 us
  blocking collectives: 59.8 us -> 57.4 us
    unnamed x21 -> x0, local copies, waits for them, and re-layouts: 5.2 us -> none
    all_to_all x2, blocking collectives: 59.8 us -> 57.4 us  [the longest x1 36.5 us: shards(): got = in_place(lax.all_to_all(channels, TM, 0, 0, tiled=True))]
    pallas_call x1, Pallas kernels: 1.76 us -> 0.18 us  [shards(): pl.pallas_call(chain_kernel, out_shape=rows, in_specs=in_vmem(2), out_spe...]
    pallas_call x1 -> x2, Pallas kernels: 12.1 us -> 11.3 us  [the longest x1 10.4 us: shards(): pl.pallas_call(relax_kernel, out_shape=(rows, pltpu.VMEM((64, LANES), jnp...]
where the time goes in v2:
time: 79.4 us; the launch traced here: 79.1 us
  blocking collectives  57.4 us (72%)
  Pallas kernels  12.2 us (15%)
  starting transfers between devices  5.48 us (7%)
  waiting for transfers between devices  3.4 us (4%)
    all_to_all x1, blocking collectives, shards(): got = in_place(lax.all_to_all(channels, TM, 0, 0, tiled=True))  36.5 us
    all_to_all x1, blocking collectives, shards(): back = in_place(lax.all_to_all(sent, TM, 0, 0, tiled=True))  21 us
    pallas_call x1, Pallas kernels, shards(): pl.pallas_call(relax_kernel, out_shape=(rows, pltpu.VMEM((64, LANES), jnp...  10.4 us
    ppermute x1, starting transfers between devices, shards(): other = lax.ppermute(own, 'space', [(0, 1), (1, 0)])  5.48 us
    ppermute x1, waiting for transfers between devices, shards(): other = lax.ppermute(own, 'space', [(0, 1), (1, 0)])  3.4 us
  transfers between devices with their start and end apart: 1, of which 1 were waited for; matrix products, arithmetic and copies ran while one was open for 0% of the time, Pallas kernels for 0%

profile of v2, /device:TPU:1, one launch (start us, length us, event | category | flops | bytes accessed | tf_op | source)
XLA Modules:
  0.0 79.1 jit_solution(17421106532161120650)
XLA Ops:
  0.6 0.9 %pack.1.own_ref = f32[7,16,512]{2,1,0:T(8,128)S(1)} custom-call(f32[16,512]{1,0:T(8,128)} %control.1, f32[16,512]{1,0:T(8,128)} %initial.1, f32[16,512]{1,0:T(8,128)} %diffusion.1, f32[16,512]{1,0:T(8,128)} %reaction.1, f32[16,512]{1,0:T(8,128)} %bitcast.17, f32[16,512]{1,0:T(8,128)} %bitcast.18, f32[16,512]{1,0:T(8,128)} %bitcast.19), custom_call_target="tpu_custom_call" | custom-call | tf_op jit(solution)/shard_map/pack/pallas_call | solution.py:337
  1.6 5.5 %collective-permute-start = (f32[7,16,512]{2,1,0:T(8,128)S(1)}, f32[7,16,512]{2,1,0:T(8,128)S(1)}, u32[]{:S(2)}, u32[]{:S(2)}) collective-permute-start(f32[7,16,512]{2,1,0:T(8,128)S(1)} %pack.1.own_ref), channel_id=1, source_target_pairs={{0,1},{1,0},{2,3},{3,2},{4,5},{5,4},{6,7},{7,6},{8,9},{9,8},{10,11... | collective-permute-start | bytes 688136 | tf_op jit(solution)/shard_map/ppermute | solution.py:345
  7.1 3.4 %collective-permute-done.other_ref = f32[7,16,512]{2,1,0:T(8,128)S(1)} collective-permute-done((f32[7,16,512]{2,1,0:T(8,128)S(1)}, f32[7,16,512]{2,1,0:T(8,128)S(1)}, u32[]{:S(2)}, u32[]{:S(2)}) %collective-permute-start) | collective-permute-done | bytes 229408 | tf_op jit(solution)/shard_map/ppermute | solution.py:345
  10.5 10.4 %relax.1 = (f32[256,128]{1,0:T(8,128)S(1)}, f32[64,128]{1,0:T(8,128)S(1)}) custom-call(f32[7,16,512]{2,1,0:T(8,128)S(1)} %pack.1.own_ref, f32[7,16,512]{2,1,0:T(8,128)S(1)} %collective-permute-done.other_ref), custom_call_target="tpu_custom_call" | custom-call | tf_op jit(solution)/shard_map/relax/pallas_call | solution.py:349
  20.9 36.5 %all_to_all.22 = f32[256,1,128]{2,1,0:T(1,128)S(1)} all-to-all(f32[256,1,128]{2,1,0:T(1,128)S(1)} %bitcast.16), channel_id=1, replica_groups=mesh['tm_0'=2,'tm_1'=8,'tm_2'=8,'tm_3'=2,'space'=2] {'tm_0','tm_1','tm_2..., dimensions={0} | all-to-all | bytes 262144 | tf_op jit(solution)/shard_map/all_to_all | solution.py:363
  57.3 0.2 chain.1
  57.5 21.0 %all_to_all.23 = f32[256,1,128]{2,1,0:T(1,128)S(1)} all-to-all(f32[256,1,128]{2,1,0:T(1,128)S(1)} %bitcast.15), channel_id=1, replica_groups=mesh['tm_0'=2,'tm_1'=8,'tm_2'=8,'tm_3'=2,'space'=2] {'tm_0','tm_1','tm_2..., dimensions={0} | all-to-all | bytes 262144 | tf_op jit(solution)/shard_map/all_to_all | solution.py:367
  78.5 0.6 finish.1
Async XLA Ops:
  1.6 8.9 %collective-permute-start = (f32[7,16,512]{2,1,0:T(8,128)S(1)}, f32[7,16,512]{2,1,0:T(8,128)S(1)}, u32[]{:S(2)}, u32[]{:S(2)}) collective-permute-start(f32[7,16,512]{2,1,0:T(8,128)S(1)} %pack.1.own_ref), channel_id=1, source_target_pairs={{0,1},{1,0},{2,3},{3,2},{4,5},{5,4},{6,7},{7,6},{8,9},{9,8},{10,11... | collective-permute-start | bytes 688136 | tf_op jit(solution)/shard_map/ppermute | solution.py:345

commit v3 on v2

--- a/solution.py
+++ b/solution.py
@@ -17,7 +17,7 @@
 PHASES = 4
 
 ENTRY, FORWARD, ADJOINT, TARGET, CONTROL, SPREAD, REACTION = range(7)
-WEIGHT, INVERSE, DAMPING, ALPHA, BETA, GAMMA, SOURCE, STATE, TOTAL, FW_LESS, AD_LESS = range(11)
+DAMPING, ALPHA, BETA, GAMMA, SOURCE, STATE, TOTAL, FW_LESS, AD_LESS = range(9)
 
 
 def tm_index():
@@ -31,51 +31,75 @@
 
 
 def each(fn, *fields):
-    return [[fn(*(f[p][t] for f in fields)) for t in range(TILES)] for p in range(PHASES)]
+    return [[fn(*cells) for cells in zip(*rows)] for rows in zip(*fields)]
 
 
 def load(ref, *at):
-    return [[ref[(*at, p, slice(None), pl.ds(t * LANES, LANES))] for t in range(TILES)] for p in range(PHASES)]
+    return [[ref[(*at, p, t)] for t in range(TILES)] for p in range(PHASES)]
 
 
 def store(value, ref, *at):
-    for p in range(PHASES):
-        for t in range(TILES):
-            ref[(*at, p, slice(None), pl.ds(t * LANES, LANES))] = value[p][t]
-
-
-def make_neighbours(space):
+    for p, row in enumerate(value):
+        for t, cell in enumerate(row):
+            ref[(*at, p, t)] = cell
+
+
+def trim(field, count):
+    return [row[count : len(row) - count] for row in field]
+
+
+def make_stencil(space):
     sub = lax.broadcasted_iota(jnp.int32, (8, LANES), 0)
     lane = lax.broadcasted_iota(jnp.int32, (8, LANES), 1)
     up_ok = sub != 4 * space
     down_ok = sub != 7 - 4 * space
     first, last = (lane == 0, lane == LANES - 1)
 
-    def neighbours(v):
-        above = [jnp.where(up_ok, pltpu.roll(v[PHASES - 1][t], 1, 0), 0.0) for t in range(TILES)]
-        below = [jnp.where(down_ok, pltpu.roll(v[0][t], 7, 0), 0.0) for t in range(TILES)]
+    def widen(field, outside_zero):
         out = []
-        for p in range(PHASES):
-            ups = v[p - 1] if p else above
-            downs = v[p + 1] if p < PHASES - 1 else below
-            right = [pltpu.roll(v[p][t], 1, 1) for t in range(TILES)]
-            left = [pltpu.roll(v[p][t], LANES - 1, 1) for t in range(TILES)]
-            row = []
-            for t in range(TILES):
-                a = jnp.where(first, right[t - 1] if t else 0.0, right[t])
-                b = jnp.where(last, left[t + 1] if t < TILES - 1 else 0.0, left[t])
-                row.append((ups[t] + downs[t]) + (a + b))
-            out.append(row)
+        for row in field:
+            left = [pltpu.roll(cell, 1, 1) for cell in row[TILES - SWEEPS :]]
+            right = [pltpu.roll(cell, LANES - 1, 1) for cell in row[:SWEEPS]]
+            if outside_zero:
+                left = [jnp.where(first, 0.0, cell) for cell in left]
+                right = [jnp.where(last, 0.0, cell) for cell in right]
+            out.append(left + row + right)
         return out
 
-    return neighbours
-
-
-def pack_kernel(control, initial, diffusion, reaction, forward, adjoint, observed, out_ref, sems):
+    def neighbours(field):
+        above = [jnp.where(up_ok, pltpu.roll(cell, 1, 0), 0.0) for cell in field[-1][1:-1]]
+        below = [jnp.where(down_ok, pltpu.roll(cell, 7, 0), 0.0) for cell in field[0][1:-1]]
+        out = []
+        for p, row in enumerate(field):
+            ups = field[p - 1][1:-1] if p else above
+            downs = field[p + 1][1:-1] if p < PHASES - 1 else below
+            out.append([(u + d) + (a + b) for u, d, a, b in zip(ups, downs, row[:-2], row[2:])])
+        return out
+
+    return widen, neighbours
+
+
+def exact_terms(value):
+    high = value.astype(jnp.bfloat16)
+    rest = value - high.astype(jnp.float32)
+    middle = rest.astype(jnp.bfloat16)
+    low = (rest - middle.astype(jnp.float32)).astype(jnp.bfloat16)
+    return high, middle, low
+
+
+def reorder(value, selection, contracted):
+    high, middle, low = (
+        lax.dot_general(term, selection, (((1,), (contracted,)), ((), ())), preferred_element_type=jnp.float32)
+        for term in exact_terms(value)
+    )
+    return high + (middle + low)
+
+
+def pack_kernel(control, initial, diffusion, reaction, forward, adjoint, observed, out_ref, order_ref, raw, sems):
     is_last = tm_index() == SLABS - 1
 
     def copy(source, slot):
-        return pltpu.make_async_copy(source, out_ref.at[slot], sems.at[slot])
+        return pltpu.make_async_copy(source, raw.at[slot], sems.at[slot])
 
     @pl.when(is_last)
     def _():
@@ -95,15 +119,20 @@
     )
     for source, slot in rest:
         copy(source, slot).start()
+    column = lax.broadcasted_iota(jnp.int32, (LANES, COLS), 1)
+    lane = lax.broadcasted_iota(jnp.int32, (LANES, COLS), 0)
+    for t in range(TILES):
+        order_ref[t * LANES : (t + 1) * LANES, :] = jnp.where(column == TILES * lane + t, 1.0, 0.0).astype(jnp.bfloat16)
     copy(forward, ENTRY).wait()
     for source, slot in rest:
         copy(source, slot).wait()
-
-
-def relax_kernel(own_ref, other_ref, chan_ref, keep_ref, raw, grid, field, points, coarse_points):
+    packed = reorder(raw[...].reshape(7 * ROWS, COLS), order_ref[...], 1)
+    out_ref[...] = packed.reshape(7, ROWS, COLS)
+
+
+def relax_kernel(own_ref, other_ref, chan_ref, keep_ref, raw, grid, field, wide, points, coarse_points):
     slab = tm_index()
-    space = space_index()
-    neighbours = make_neighbours(space)
+    widen, neighbours = make_stencil(space_index())
     is_last = slab == SLABS - 1
     not_last = jnp.where(is_last, 0.0, 1.0)
     not_first = jnp.where(slab == 0, 0.0, 1.0)
@@ -116,41 +145,54 @@
     for n in range(7):
         for p in range(PHASES):
             for t in range(TILES):
-                grid[n, p, :, pl.ds(t * LANES, LANES)] = raw[n, t, pl.ds(p, 8, stride=PHASES), :]
+                grid[n, p, t] = raw[n, t, pl.ds(p, 8, stride=PHASES), :]
 
     spread, reaction = (load(grid, SPREAD), load(grid, REACTION))
     inverse = each(lambda s, r: 1.0 / (1.0 + 4.0 * s + r), spread, reaction)
-    store(inverse, field, INVERSE)
-    store(each(lambda s, i: s * i, spread, inverse), field, WEIGHT)
-    store(each(lambda r: 1.0 / (1.0 + COARSEN * r), reaction), field, DAMPING)
+    store(widen(inverse, True), wide, 0)
+    store(widen(each(jnp.multiply, spread, inverse), True), wide, 1)
+    damping = each(lambda r: 1.0 / (1.0 + COARSEN * r), reaction)
+    store(damping, field, DAMPING)
+
+    def inverse_wide(count):
+        return [[wide[0, p, t] for t in range(SWEEPS - count, SWEEPS + TILES + count)] for p in range(PHASES)]
+
+    def weight_wide(count):
+        return [[wide[1, p, t] for t in range(SWEEPS - count, SWEEPS + TILES + count)] for p in range(PHASES)]
 
     def forward_step(right_side):
-        weight, scaled = (load(field, WEIGHT), each(lambda r, i: r * i, right_side, load(field, INVERSE)))
-        v = right_side
-        for _ in range(SWEEPS):
-            v = each(lambda s, w, n: s + w * n, scaled, weight, neighbours(v))
+        v = widen(right_side, True)
+        scaled = each(jnp.multiply, inverse_wide(SWEEPS - 1), trim(v, 1))
+        for n in range(SWEEPS):
+            v = each(
+                lambda s, w, q: s + w * q, trim(scaled, n), weight_wide(SWEEPS - 1 - n), neighbours(v)
+            )
         return v
 
     def adjoint_step(y):
-        weight = load(field, WEIGHT)
-        carried, summed = (y, y)
-        for _ in range(SWEEPS - 1):
-            carried = neighbours(each(jnp.multiply, weight, carried))
-            summed = each(jnp.add, summed, carried)
-        final = neighbours(each(jnp.multiply, weight, carried))
-        return each(lambda s, i, f: s * i + f, summed, load(field, INVERSE), final)
+        carried, summed = (widen(y, False), y)
+        for n in range(SWEEPS - 1):
+            carried = neighbours(each(jnp.multiply, weight_wide(SWEEPS - n), carried))
+            summed = each(jnp.add, summed, trim(carried, SWEEPS - 1 - n))
+        final = neighbours(each(jnp.multiply, weight_wide(1), carried))
+        return each(lambda s, i, f: s * i + f, summed, inverse_wide(0), final)
 
     store(load(grid, ENTRY), field, STATE)
+    store(load(grid, ADJOINT), field, BETA)
+    store(each(lambda g: g / COARSEN, load(grid, FORWARD)), field, GAMMA)
 
     def forward_body(i, _):
         v = forward_step(each(jnp.add, load(field, STATE), load(grid, CONTROL)))
+        beta = adjoint_step(load(field, BETA))
+        gamma = adjoint_step(each(lambda a, o: a - o / COARSEN, load(field, GAMMA), load(grid, TARGET)))
         store(v, field, STATE)
         store(v, points, i)
+        store(beta, field, BETA)
+        store(gamma, field, GAMMA)
         return 0
 
     lax.fori_loop(0, COARSEN, forward_body, 0)
 
-    damping = load(field, DAMPING)
     forward_less = jnp.where(is_last, SLABS - 1, SLABS - 2 - slab)
     adjoint_less = jnp.maximum(slab - 1, 0)
     for slot, count in ((FW_LESS, forward_less), (AD_LESS, adjoint_less)):
@@ -164,40 +206,30 @@
                 power = each(lambda q: q * q, power)
         store(total, field, slot)
 
-    push = each(
-        lambda f, d, g: f - not_last * (d * g), load(field, STATE), damping, load(grid, FORWARD)
-    )
+    push = each(lambda f, d, g: f - not_last * (d * g), load(field, STATE), load(field, DAMPING), load(grid, FORWARD))
     store(push, field, SOURCE)
     store(
         each(lambda w, u, e: w * u + (1.0 - not_last) * e, load(field, FW_LESS), push, load(grid, ENTRY)),
         field,
         STATE,
     )
-    store(each(jnp.zeros_like, damping), field, ALPHA)
-    store(load(grid, ADJOINT), field, BETA)
-    store(each(lambda g: g / COARSEN, load(grid, FORWARD)), field, GAMMA)
+    store(each(jnp.zeros_like, push), field, ALPHA)
 
     def adjoint_body(n, _):
-        at = COARSEN - 1 - n
-        share = jnp.where(n == 0, 0.0, 1.0 / COARSEN)
-        store(adjoint_step(each(lambda a, f: a + share * f, load(field, ALPHA), load(points, at))), field, ALPHA)
-        store(adjoint_step(load(field, BETA)), field, BETA)
-        store(
-            adjoint_step(each(lambda a, o: a - o / COARSEN, load(field, GAMMA), load(grid, TARGET))), field, GAMMA
-        )
+        at = COARSEN - 2 - n
+        alpha = adjoint_step(each(lambda a, f: a + f / COARSEN, load(field, ALPHA), load(points, at)))
         v = forward_step(each(jnp.add, load(field, STATE), load(grid, CONTROL)))
+        store(alpha, field, ALPHA)
         store(v, field, STATE)
         store(v, coarse_points, n)
         return 0
 
-    lax.fori_loop(0, COARSEN, adjoint_body, 0)
+    lax.fori_loop(0, COARSEN - 1, adjoint_body, 0)
 
     damping = load(field, DAMPING)
     alpha, beta, gamma = (load(field, ALPHA), load(field, BETA), load(field, GAMMA))
     keep = each(lambda g, d, a: g + not_last * (d * a), gamma, damping, alpha)
-    pull = each(
-        lambda k, d, g, b: d * (k - g) + b, keep, damping, load(grid, ADJOINT), beta
-    )
+    pull = each(lambda k, d, g, b: d * (k - g) + b, keep, damping, load(grid, ADJOINT), beta)
     push = load(field, SOURCE)
     less = load(field, AD_LESS)
     store(
@@ -235,11 +267,10 @@
     for n, slot in enumerate((SOURCE, BETA, ALPHA, TOTAL)):
         for p in range(PHASES):
             for t in range(TILES):
-                block = field[slot, p, 0:4, pl.ds(t * LANES, LANES)]
-                chan_ref[pl.ds((n * TILES + t) * ROWS + p, 4, stride=PHASES), :] = block
+                chan_ref[pl.ds((n * TILES + t) * ROWS + p, 4, stride=PHASES), :] = field[slot, p, t, 0:4, :]
     for p in range(PHASES):
         for t in range(TILES):
-            keep_ref[pl.ds(t * ROWS + p, 4, stride=PHASES), :] = field[STATE, p, 0:4, pl.ds(t * LANES, LANES)]
+            keep_ref[pl.ds(t * ROWS + p, 4, stride=PHASES), :] = field[STATE, p, t, 0:4, :]
 
 
 def chain_kernel(got_ref, own_ref, out_ref):
@@ -312,13 +343,16 @@
             out_ref[pl.ds(8 * i, 8), :] = total
 
 
-def finish_kernel(got_ref, keep_ref, forward_ref, adjoint_ref, gradient_ref):
-    for t in range(TILES):
-        cols = pl.ds(t * LANES, LANES)
-        forward, scanned, passed, gradient = (got_ref[pl.ds(64 * n + t * ROWS, ROWS), :] for n in range(4))
-        forward_ref[:, cols] = forward
-        adjoint_ref[:, cols] = scanned + (passed + keep_ref[pl.ds(t * ROWS, ROWS), :])
-        gradient_ref[:, cols] = gradient
+def finish_kernel(got_ref, keep_ref, order_ref, forward_ref, adjoint_ref, gradient_ref):
+    def rows(ref, n):
+        return jnp.concatenate([ref[pl.ds((n * TILES + t) * ROWS, ROWS), :] for t in range(TILES)], 1)
+
+    adjoint = rows(got_ref, 1) + (rows(got_ref, 2) + rows(keep_ref, 0))
+    parts = jnp.concatenate([rows(got_ref, 0), adjoint, rows(got_ref, 3)], 0)
+    parts = reorder(parts, order_ref[...], 0)
+    forward_ref[...] = parts[0:ROWS]
+    adjoint_ref[...] = parts[ROWS : 2 * ROWS]
+    gradient_ref[...] = parts[2 * ROWS : 3 * ROWS]
 
 
 def in_vmem(count):
@@ -330,16 +364,27 @@
 
 
 def field_shape(*lead):
-    return pltpu.VMEM((*lead, PHASES, 8, COLS), jnp.float32)
+    return pltpu.VMEM((*lead, PHASES, TILES, 8, LANES), jnp.float32)
+
+
+def relax_scratch():
+    return [
+        pltpu.VMEM((7, TILES, 2 * ROWS, LANES), jnp.float32),
+        field_shape(7),
+        field_shape(9),
+        pltpu.VMEM((2, PHASES, TILES + 2 * SWEEPS, 8, LANES), jnp.float32),
+        field_shape(COARSEN),
+        field_shape(COARSEN - 1),
+    ]
 
 
 def shards(control, initial, diffusion, reaction, forward_guess, adjoint_guess, observed):
-    own = pl.pallas_call(
+    own, order = pl.pallas_call(
         pack_kernel,
-        out_shape=pltpu.VMEM((7, ROWS, COLS), jnp.float32),
+        out_shape=(pltpu.VMEM((7, ROWS, COLS), jnp.float32), pltpu.VMEM((COLS, COLS), jnp.bfloat16)),
         in_specs=[pl.BlockSpec(memory_space=pl.ANY)] * 7,
-        out_specs=in_vmem(1)[0],
-        scratch_shapes=[pltpu.SemaphoreType.DMA((7,))],
+        out_specs=in_vmem(2),
+        scratch_shapes=[pltpu.VMEM((7, ROWS, COLS), jnp.float32), pltpu.SemaphoreType.DMA((7,))],
         name="pack",
     )(control, initial, diffusion, reaction, forward_guess[0], adjoint_guess[0], observed[0])
     other = lax.ppermute(own, "space", [(0, 1), (1, 0)])
@@ -351,13 +396,7 @@
         out_shape=(rows, pltpu.VMEM((64, LANES), jnp.float32)),
         in_specs=in_vmem(2),
         out_specs=in_vmem(2),
-        scratch_shapes=[
-            pltpu.VMEM((7, TILES, 2 * ROWS, LANES), jnp.float32),
-            field_shape(7),
-            field_shape(11),
-            field_shape(COARSEN),
-            field_shape(COARSEN),
-        ],
+        scratch_shapes=relax_scratch(),
         name="relax",
     )(own, other)
     got = in_place(lax.all_to_all(channels, TM, 0, 0, tiled=True))
@@ -365,10 +404,10 @@
         chain_kernel, out_shape=rows, in_specs=in_vmem(2), out_specs=in_vmem(1)[0], name="chain"
     )(got, own)
     back = in_place(lax.all_to_all(sent, TM, 0, 0, tiled=True))
-    keep = in_place(keep)
+    keep, order = in_place(keep), in_place(order)
     forward_states, adjoint_states, gradient = pl.pallas_call(
-        finish_kernel, out_shape=(block, block, block), in_specs=in_vmem(2), out_specs=in_vmem(3), name="finish"
-    )(back, keep)
+        finish_kernel, out_shape=(block, block, block), in_specs=in_vmem(3), out_specs=in_vmem(3), name="finish"
+    )(back, keep, order)
     return (forward_states[None], adjoint_states[None], gradient)
 
 

time: 79.4 us -> 74.6 us (0.940)
  Pallas kernels: 12.2 us -> 7.28 us
    pallas_call x1, Pallas kernels: 10.4 us -> 4.55 us  [shards(): pl.pallas_call(relax_kernel, out_shape=(rows, pltpu.VMEM((64, LANES), jnp...]
where the time goes in v3:
time: 74.6 us; the launch traced here: 74.2 us
  blocking collectives  57.4 us (77%)
  Pallas kernels  7.28 us (10%)
  starting transfers between devices  5.48 us (7%)
  waiting for transfers between devices  3.4 us (5%)
    all_to_all x1, blocking collectives, shards(): got = in_place(lax.all_to_all(channels, TM, 0, 0, tiled=True))  36.5 us
    all_to_all x1, blocking collectives, shards(): back = in_place(lax.all_to_all(sent, TM, 0, 0, tiled=True))  21 us
    ppermute x1, starting transfers between devices, shards(): other = lax.ppermute(own, 'space', [(0, 1), (1, 0)])  5.48 us
    pallas_call x1, Pallas kernels, shards(): pl.pallas_call(relax_kernel, out_shape=(rows, pltpu.VMEM((64, LANES), jnp...  4.55 us
    ppermute x1, waiting for transfers between devices, shards(): other = lax.ppermute(own, 'space', [(0, 1), (1, 0)])  3.4 us
    pallas_call x1, Pallas kernels, shards(): pl.pallas_call(pack_kernel, out_shape=(pltpu.VMEM((7, ROWS, COLS), jnp.fl...  1.56 us
  transfers between devices with their start and end apart: 1, of which 1 were waited for; matrix products, arithmetic and copies ran while one was open for 0% of the time, Pallas kernels for 0%

profile of v3, /device:TPU:1, one launch (start us, length us, event | category | flops | bytes accessed | tf_op | source)
XLA Modules:
  0.0 74.2 jit_solution(10489158591588869671)
XLA Ops:
  0.6 1.6 %pack.1 = (f32[7,16,512]{2,1,0:T(8,128)S(1)}, bf16[512,512]{1,0:T(8,128)(2,1)S(1)}) custom-call(f32[16,512]{1,0:T(8,128)} %control.1, f32[16,512]{1,0:T(8,128)} %initial.1, f32[16,512]{1,0:T(8,128)} %diffusion.1, f32[16,512]{1,0:T(8,128)} %reaction.1, f32[16,512]{1,0:T(8,128)} %bitcast.17, f32[16,512]{1,0:T(8,128)} %bitcast.18, f32[16,512]{1,0:T(8,128)} %bitcast.19), custom_call_target="tpu_custom_call" | custom-call | tf_op jit(solution)/shard_map/pack/pallas_call | solution.py:382
  2.2 5.5 %collective-permute-start = (f32[7,16,512]{2,1,0:T(8,128)S(1)}, f32[7,16,512]{2,1,0:T(8,128)S(1)}, u32[]{:S(2)}, u32[]{:S(2)}) collective-permute-start(f32[7,16,512]{2,1,0:T(8,128)S(1)} %get-tuple-element.10.own_ref), channel_id=1, source_target_pairs={{0,1},{1,0},{2,3},{3,2},{4,5},{5,4},{6,7},{7,6},{8,9},{9,8},{10,11... | collective-permute-start | bytes 688136 | tf_op jit(solution)/shard_map/ppermute | solution.py:390
  7.7 3.4 %collective-permute-done.other_ref = f32[7,16,512]{2,1,0:T(8,128)S(1)} collective-permute-done((f32[7,16,512]{2,1,0:T(8,128)S(1)}, f32[7,16,512]{2,1,0:T(8,128)S(1)}, u32[]{:S(2)}, u32[]{:S(2)}) %collective-permute-start) | collective-permute-done | bytes 229408 | tf_op jit(solution)/shard_map/ppermute | solution.py:390
  11.1 4.6 %relax.1 = (f32[256,128]{1,0:T(8,128)S(1)}, f32[64,128]{1,0:T(8,128)S(1)}) custom-call(f32[7,16,512]{2,1,0:T(8,128)S(1)} %get-tuple-element.10.own_ref, f32[7,16,512]{2,1,0:T(8,128)S(1)} %collective-permute-done.other_ref), custom_call_target="tpu_custom_call" | custom-call | tf_op jit(solution)/shard_map/relax/pallas_call | solution.py:394
  15.6 36.5 %all_to_all.22 = f32[256,1,128]{2,1,0:T(1,128)S(1)} all-to-all(f32[256,1,128]{2,1,0:T(1,128)S(1)} %bitcast.16), channel_id=1, replica_groups=mesh['tm_0'=2,'tm_1'=8,'tm_2'=8,'tm_3'=2,'space'=2] {'tm_0','tm_1','tm_2..., dimensions={0} | all-to-all | bytes 262144 | tf_op jit(solution)/shard_map/all_to_all | solution.py:402
  52.1 0.2 chain.1
  52.3 21.0 %all_to_all.23 = f32[256,1,128]{2,1,0:T(1,128)S(1)} all-to-all(f32[256,1,128]{2,1,0:T(1,128)S(1)} %bitcast.15), channel_id=1, replica_groups=mesh['tm_0'=2,'tm_1'=8,'tm_2'=8,'tm_3'=2,'space'=2] {'tm_0','tm_1','tm_2..., dimensions={0} | all-to-all | bytes 262144 | tf_op jit(solution)/shard_map/all_to_all | solution.py:406
  73.3 1.0 %finish.1 = (f32[16,512]{1,0:T(8,128)}, f32[16,512]{1,0:T(8,128)}, f32[16,512]{1,0:T(8,128)}) custom-call(f32[256,128]{1,0:T(8,128)S(1)} %bitcast.13, f32[64,128]{1,0:T(8,128)S(1)} %get-tuple-element.12.keep_ref, bf16[512,512]{1,0:T(8,128)(2,1)S(1)} %get-tuple-element.13.order_ref), custom_call_target="tpu_custom_call" | custom-call | tf_op jit(solution)/shard_map/finish/pallas_call | solution.py:408
Async XLA Ops:
  2.2 8.9 %collective-permute-start = (f32[7,16,512]{2,1,0:T(8,128)S(1)}, f32[7,16,512]{2,1,0:T(8,128)S(1)}, u32[]{:S(2)}, u32[]{:S(2)}) collective-permute-start(f32[7,16,512]{2,1,0:T(8,128)S(1)} %get-tuple-element.10.own_ref), channel_id=1, source_target_pairs={{0,1},{1,0},{2,3},{3,2},{4,5},{5,4},{6,7},{7,6},{8,9},{9,8},{10,11... | collective-permute-start | bytes 688136 | tf_op jit(solution)/shard_map/ppermute | solution.py:390

commit v4 on v3

--- a/solution.py
+++ b/solution.py
@@ -130,9 +130,10 @@
     out_ref[...] = packed.reshape(7, ROWS, COLS)
 
 
-def relax_kernel(own_ref, other_ref, chan_ref, keep_ref, raw, grid, field, wide, points, coarse_points):
+def relax_kernel(own_ref, both_ref, chan_ref, keep_ref, raw, grid, field, wide, points, coarse_points):
     slab = tm_index()
-    widen, neighbours = make_stencil(space_index())
+    space = space_index()
+    widen, neighbours = make_stencil(space)
     is_last = slab == SLABS - 1
     not_last = jnp.where(is_last, 0.0, 1.0)
     not_first = jnp.where(slab == 0, 0.0, 1.0)
@@ -141,7 +142,7 @@
         for t in range(TILES):
             cols = pl.ds(t * LANES, LANES)
             raw[n, t, 0:ROWS, :] = own_ref[n, :, cols]
-            raw[n, t, ROWS : 2 * ROWS, :] = other_ref[n, :, cols]
+            raw[n, t, ROWS : 2 * ROWS, :] = both_ref[1 - space, n, :, cols]
     for n in range(7):
         for p in range(PHASES):
             for t in range(TILES):
@@ -387,8 +388,8 @@
         scratch_shapes=[pltpu.VMEM((7, ROWS, COLS), jnp.float32), pltpu.SemaphoreType.DMA((7,))],
         name="pack",
     )(control, initial, diffusion, reaction, forward_guess[0], adjoint_guess[0], observed[0])
-    other = lax.ppermute(own, "space", [(0, 1), (1, 0)])
-    own, other = in_place(own), in_place(other)
+    both = in_place(lax.all_gather(own, "space", axis=0))
+    own = in_place(own)
     block = jax.ShapeDtypeStruct((ROWS, COLS), jnp.float32)
     rows = pltpu.VMEM((SLABS, LANES), jnp.float32)
     channels, keep = pl.pallas_call(
@@ -398,7 +399,7 @@
         out_specs=in_vmem(2),
         scratch_shapes=relax_scratch(),
         name="relax",
-    )(own, other)
+    )(own, both)
     got = in_place(lax.all_to_all(channels, TM, 0, 0, tiled=True))
     sent = pl.pallas_call(
         chain_kernel, out_shape=rows, in_specs=in_vmem(2), out_specs=in_vmem(1)[0], name="chain"

time: 74.6 us -> 73.3 us (0.983)
  blocking collectives: 57.4 us -> 65.1 us
  starting transfers between devices: 5.48 us -> 0 us
  waiting for transfers between devices: 3.4 us -> 0 us
    all_gather x0 -> x1, blocking collectives: none -> 7.65 us  [shards(): both = in_place(lax.all_gather(own, 'space', axis=0))]
    ppermute x1 -> x0, starting transfers between devices: 5.48 us -> none  [shards(): other = lax.ppermute(own, 'space', [(0, 1), (1, 0)])]
    ppermute x1 -> x0, waiting for transfers between devices: 3.4 us -> none  [shards(): other = lax.ppermute(own, 'space', [(0, 1), (1, 0)])]
  transfers between devices with their start and end apart: 1 -> 0, of which waited for: 1 -> 0; matrix products, arithmetic and copies ran while one was open for 0% -> 0% of each run, Pallas kernels for 0% -> 0%
where the time goes in v4:
time: 73.3 us; the launch traced here: 73 us
  blocking collectives  65.1 us (89%)
  Pallas kernels  7.28 us (10%)
    all_to_all x1, blocking collectives, shards(): got = in_place(lax.all_to_all(channels, TM, 0, 0, tiled=True))  36.5 us
    all_to_all x1, blocking collectives, shards(): back = in_place(lax.all_to_all(sent, TM, 0, 0, tiled=True))  21 us
    all_gather x1, blocking collectives, shards(): both = in_place(lax.all_gather(own, 'space', axis=0))  7.65 us
    pallas_call x1, Pallas kernels, shards(): pl.pallas_call(relax_kernel, out_shape=(rows, pltpu.VMEM((64, LANES), jnp...  4.56 us
    pallas_call x1, Pallas kernels, shards(): pl.pallas_call(pack_kernel, out_shape=(pltpu.VMEM((7, ROWS, COLS), jnp.fl...  1.56 us

profile of v4, /device:TPU:1, one launch (start us, length us, event | category | flops | bytes accessed | tf_op | source)
XLA Modules:
  0.0 73.0 jit_solution(13933630666936780027)
XLA Ops:
  0.6 1.6 %pack.1 = (f32[7,16,512]{2,1,0:T(8,128)S(1)}, bf16[512,512]{1,0:T(8,128)(2,1)S(1)}) custom-call(f32[16,512]{1,0:T(8,128)} %control.1, f32[16,512]{1,0:T(8,128)} %initial.1, f32[16,512]{1,0:T(8,128)} %diffusion.1, f32[16,512]{1,0:T(8,128)} %reaction.1, f32[16,512]{1,0:T(8,128)} %bitcast.19, f32[16,512]{1,0:T(8,128)} %bitcast.20, f32[16,512]{1,0:T(8,128)} %bitcast.21), custom_call_target="tpu_custom_call" | custom-call | tf_op jit(solution)/shard_map/pack/pallas_call | solution.py:383
  2.2 7.6 %all-gather = f32[14,16,512]{2,1,0:T(8,128)S(1)} all-gather(f32[7,16,512]{2,1,0:T(8,128)S(1)} %get-tuple-element.10.own_ref), channel_id=2, replica_groups=mesh['tm_0'=2,'tm_1'=8,'tm_2'=8,'tm_3'=2,'space'=2] {'space'}, dimensions={0}, use_global_device_ids=true | all-gather | bytes 688128 | tf_op jit(solution)/shard_map/all_gather | solution.py:391
  9.8 4.6 %relax.1 = (f32[256,128]{1,0:T(8,128)S(1)}, f32[64,128]{1,0:T(8,128)S(1)}) custom-call(f32[7,16,512]{2,1,0:T(8,128)S(1)} %get-tuple-element.10.own_ref, f32[2,7,16,512]{3,2,1,0:T(8,128)S(1)} %bitcast.14), custom_call_target="tpu_custom_call" | custom-call | tf_op jit(solution)/shard_map/relax/pallas_call | solution.py:395
  14.4 36.5 %all_to_all.22 = f32[256,1,128]{2,1,0:T(1,128)S(1)} all-to-all(f32[256,1,128]{2,1,0:T(1,128)S(1)} %bitcast.18), channel_id=1, replica_groups=mesh['tm_0'=2,'tm_1'=8,'tm_2'=8,'tm_3'=2,'space'=2] {'tm_0','tm_1','tm_2..., dimensions={0} | all-to-all | bytes 262144 | tf_op jit(solution)/shard_map/all_to_all | solution.py:403
  50.9 0.2 chain.1
  51.1 21.0 %all_to_all.23 = f32[256,1,128]{2,1,0:T(1,128)S(1)} all-to-all(f32[256,1,128]{2,1,0:T(1,128)S(1)} %bitcast.17), channel_id=1, replica_groups=mesh['tm_0'=2,'tm_1'=8,'tm_2'=8,'tm_3'=2,'space'=2] {'tm_0','tm_1','tm_2..., dimensions={0} | all-to-all | bytes 262144 | tf_op jit(solution)/shard_map/all_to_all | solution.py:407
  72.0 1.0 %finish.1 = (f32[16,512]{1,0:T(8,128)}, f32[16,512]{1,0:T(8,128)}, f32[16,512]{1,0:T(8,128)}) custom-call(f32[256,128]{1,0:T(8,128)S(1)} %bitcast.15, f32[64,128]{1,0:T(8,128)S(1)} %get-tuple-element.12.keep_ref, bf16[512,512]{1,0:T(8,128)(2,1)S(1)} %get-tuple-element.13.order_ref), custom_call_target="tpu_custom_call" | custom-call | tf_op jit(solution)/shard_map/finish/pallas_call | solution.py:409

commit v5 on v4

--- a/solution.py
+++ b/solution.py
@@ -15,6 +15,8 @@
 LANES = 128
 TILES = COLS // LANES
 PHASES = 4
+BLOCK = 16
+BLOCKS = SLABS // BLOCK
 
 ENTRY, FORWARD, ADJOINT, TARGET, CONTROL, SPREAD, REACTION = range(7)
 DAMPING, ALPHA, BETA, GAMMA, SOURCE, STATE, TOTAL, FW_LESS, AD_LESS = range(9)
@@ -70,10 +72,14 @@
         above = [jnp.where(up_ok, pltpu.roll(cell, 1, 0), 0.0) for cell in field[-1][1:-1]]
         below = [jnp.where(down_ok, pltpu.roll(cell, 7, 0), 0.0) for cell in field[0][1:-1]]
         out = []
-        for p, row in enumerate(field):
-            ups = field[p - 1][1:-1] if p else above
-            downs = field[p + 1][1:-1] if p < PHASES - 1 else below
-            out.append([(u + d) + (a + b) for u, d, a, b in zip(ups, downs, row[:-2], row[2:])])
+        pairs = [[u + a for u, a in zip(above, field[0][:-2])]]
+        for p in range(1, PHASES):
+            pairs.append([u + a for u, a in zip(field[p - 1][1:], field[p][:-1])])
+        pairs.append([b + d for b, d in zip(field[-1][2:], below)])
+        for p in range(PHASES):
+            upper = pairs[p][:-1] if p else pairs[p]
+            lower = pairs[p + 1][1:] if p < PHASES - 1 else pairs[p + 1]
+            out.append([x + y for x, y in zip(upper, lower)])
         return out
 
     return widen, neighbours
@@ -87,15 +93,15 @@
     return high, middle, low
 
 
-def reorder(value, selection, contracted):
+def reorder(value, selection):
     high, middle, low = (
-        lax.dot_general(term, selection, (((1,), (contracted,)), ((), ())), preferred_element_type=jnp.float32)
+        jnp.dot(term, selection, preferred_element_type=jnp.float32)
         for term in exact_terms(value)
     )
     return high + (middle + low)
 
 
-def pack_kernel(control, initial, diffusion, reaction, forward, adjoint, observed, out_ref, order_ref, raw, sems):
+def pack_kernel(control, initial, diffusion, reaction, forward, adjoint, observed, out_ref, order_ref, raw, into, sems):
     is_last = tm_index() == SLABS - 1
 
     def copy(source, slot):
@@ -119,14 +125,16 @@
     )
     for source, slot in rest:
         copy(source, slot).start()
-    column = lax.broadcasted_iota(jnp.int32, (LANES, COLS), 1)
-    lane = lax.broadcasted_iota(jnp.int32, (LANES, COLS), 0)
+    column, lane = (lax.broadcasted_iota(jnp.int32, (LANES, COLS), d) for d in (1, 0))
     for t in range(TILES):
         order_ref[t * LANES : (t + 1) * LANES, :] = jnp.where(column == TILES * lane + t, 1.0, 0.0).astype(jnp.bfloat16)
+    column, lane = (lax.broadcasted_iota(jnp.int32, (COLS, LANES), d) for d in (0, 1))
+    for t in range(TILES):
+        into[:, t * LANES : (t + 1) * LANES] = jnp.where(column == TILES * lane + t, 1.0, 0.0).astype(jnp.bfloat16)
     copy(forward, ENTRY).wait()
     for source, slot in rest:
         copy(source, slot).wait()
-    packed = reorder(raw[...].reshape(7 * ROWS, COLS), order_ref[...], 1)
+    packed = reorder(raw[...].reshape(7 * ROWS, COLS), into[...])
     out_ref[...] = packed.reshape(7, ROWS, COLS)
 
 
@@ -225,7 +233,7 @@
         store(v, coarse_points, n)
         return 0
 
-    lax.fori_loop(0, COARSEN - 1, adjoint_body, 0)
+    lax.fori_loop(0, COARSEN - 1, adjoint_body, 0, unroll=True)
 
     damping = load(field, DAMPING)
     alpha, beta, gamma = (load(field, ALPHA), load(field, BETA), load(field, GAMMA))
@@ -263,94 +271,101 @@
         )
         return 0
 
-    lax.fori_loop(0, COARSEN - 1, gradient_body, 0)
+    lax.fori_loop(0, COARSEN - 1, gradient_body, 0, unroll=True)
 
     for n, slot in enumerate((SOURCE, BETA, ALPHA, TOTAL)):
         for p in range(PHASES):
             for t in range(TILES):
-                chan_ref[pl.ds((n * TILES + t) * ROWS + p, 4, stride=PHASES), :] = field[slot, p, t, 0:4, :]
+                raw[n, t, pl.ds(p, 4, stride=PHASES), :] = field[slot, p, t, 0:4, :]
+    for n in range(4):
+        for t in range(TILES):
+            for h in range(2):
+                chan_ref[2 * t + h, n] = raw[n, t, 8 * h : 8 * h + 8, :]
     for p in range(PHASES):
         for t in range(TILES):
             keep_ref[pl.ds(t * ROWS + p, 4, stride=PHASES), :] = field[STATE, p, t, 0:4, :]
 
 
-def chain_kernel(got_ref, own_ref, out_ref):
-    owner = tm_index()
-    role = owner // 64
-    cell = owner % 64
-    tile = cell // ROWS
-    row = own_ref[REACTION, pl.ds(cell % ROWS, 1), :]
-    reaction = row[:, 0:LANES]
+def owned_damping(own_ref):
+    owner = lax.axis_index("tm_2")
+    rows = own_ref[REACTION, pl.ds(pl.multiple_of(8 * (owner % 2), 8), 8), :]
+    reaction = rows[:, 0:LANES]
     for t in range(1, TILES):
-        reaction = jnp.where(tile == t, row[:, t * LANES : (t + 1) * LANES], reaction)
-    d = jnp.broadcast_to(1.0 / (1.0 + COARSEN * reaction), (8, LANES))
-    length = SLABS // 8
-    sub = lax.broadcasted_iota(jnp.int32, (8, LANES), 0)
-    d32 = d
-    for _ in range(5):
-        d32 = d32 * d32
-    d64 = d32 * d32
-    d128 = d64 * d64
-
-    def strided(i):
-        return pl.ds(i, 8, stride=length)
-
-    @pl.when(role == 0)
-    def _():
-        x = pltpu.roll(got_ref[strided(length - 1), :], 1, 0)
-        local = [x]
-        for i in range(1, length):
-            x = d * x + got_ref[strided(i - 1), :]
-            local.append(x)
-        c = x
-        c = c + jnp.where(sub >= 1, d32 * pltpu.roll(c, 1, 0), 0.0)
-        c = c + jnp.where(sub >= 2, d64 * pltpu.roll(c, 2, 0), 0.0)
-        c = c + jnp.where(sub >= 4, d128 * pltpu.roll(c, 4, 0), 0.0)
-        c = jnp.where(sub >= 1, pltpu.roll(c, 1, 0), 0.0)
-        for i in range(length):
-            c = d * c
-            out_ref[strided(i), :] = local[i] + c
-
-    @pl.when(role == 1)
-    def _():
-        x = jnp.where(sub == 7, 0.0, pltpu.roll(got_ref[strided(0), :], 7, 0))
-        local = [x]
-        for i in range(length - 2, -1, -1):
-            x = d * x + got_ref[strided(i + 1), :]
-            local.append(x)
-        c = x
-        c = c + jnp.where(sub < 7, d32 * pltpu.roll(c, 7, 0), 0.0)
-        c = c + jnp.where(sub < 6, d64 * pltpu.roll(c, 6, 0), 0.0)
-        c = c + jnp.where(sub < 4, d128 * pltpu.roll(c, 4, 0), 0.0)
-        c = jnp.where(sub < 7, pltpu.roll(c, 7, 0), 0.0)
-        for n in range(length):
-            c = d * c
-            out_ref[strided(length - 1 - n), :] = local[n] + c
-
-    @pl.when(role == 2)
-    def _():
-        out_ref[strided(0), :] = pltpu.roll(got_ref[strided(length - 1), :], 1, 0)
-        for i in range(1, length):
-            out_ref[strided(i), :] = got_ref[strided(i - 1), :]
-
-    @pl.when(role == 3)
-    def _():
-        parts = [got_ref[pl.ds(8 * i, 8), :] for i in range(length)]
-        while len(parts) > 1:
-            parts = [a + b for a, b in zip(parts[::2], parts[1::2])]
-        total = jnp.sum(parts[0], axis=0, keepdims=True) * (1.0 / (COARSEN * SLABS))
-        total = jnp.broadcast_to(total, (8, LANES))
-        for i in range(length):
-            out_ref[pl.ds(8 * i, 8), :] = total
+        reaction = jnp.where(owner // 2 == t, rows[:, t * LANES : (t + 1) * LANES], reaction)
+    return 1.0 / (1.0 + COARSEN * reaction)
+
+
+def block_kernel(got_ref, own_ref, totals_ref, local_ref):
+    d = owned_damping(own_ref)
+    block = lax.axis_index("tm_0") * 8 + lax.axis_index("tm_1")
+    even = lax.axis_index("tm_3") == 0
+
+    def source(n, i):
+        return got_ref[i % 2, i // 2, n]
+
+    zero = jnp.zeros_like(d)
+    forward, adjoint, shifted = ([zero], [zero], [zero])
+    for i in range(BLOCK):
+        forward.append(d * forward[i] + source(0, i))
+        shifted.append(source(2, i))
+    for i in range(BLOCK - 1, -1, -1):
+        adjoint.append(d * adjoint[-1] + source(1, i))
+    adjoint = adjoint[::-1][1:]
+    gradient = [source(3, i) for i in range(BLOCK)]
+    while len(gradient) > 1:
+        gradient = [a + b for a, b in zip(gradient[::2], gradient[1::2])]
+    first = jnp.where(block == BLOCKS - 1, source(0, BLOCK - 1), forward[BLOCK])
+    whole = d * adjoint[0] + source(1, 0)
+    totals = (first, whole, shifted[BLOCK], gradient[0])
+    for b in range(BLOCKS):
+        for n, value in enumerate(totals):
+            totals_ref[b, n] = value
+    for y in range(BLOCK // 2):
+        for n, values in enumerate((forward, adjoint, shifted)):
+            local_ref[y, n] = jnp.where(even, values[2 * y], values[2 * y + 1])
+
+
+def spread_kernel(totals_ref, local_ref, own_ref, out_ref):
+    d = owned_damping(own_ref)
+    block = lax.axis_index("tm_0") * 8 + lax.axis_index("tm_1")
+    even = lax.axis_index("tm_3") == 0
+    d2 = d * d
+    d4 = d2 * d2
+    d16 = (d4 * d4) * (d4 * d4)
+    entry = totals_ref[BLOCKS - 1, 0]
+    for b in range(BLOCKS - 1):
+        entry = jnp.where(b < block, d16 * entry + totals_ref[b, 0], entry)
+    after = jnp.zeros_like(d)
+    for b in range(BLOCKS - 1, 0, -1):
+        after = jnp.where(b > block, d16 * after + totals_ref[b, 1], after)
+    before = totals_ref[(block + BLOCKS - 1) % BLOCKS, 2]
+    gradient = [totals_ref[b, 3] for b in range(BLOCKS)]
+    while len(gradient) > 1:
+        gradient = [a + b for a, b in zip(gradient[::2], gradient[1::2])]
+    gradient = gradient[0] * (1.0 / (COARSEN * SLABS))
+    entry = jnp.where(even, entry, d * entry)
+    after = jnp.where(even, d * after, after)
+    half = BLOCK // 2
+    for y in range(half):
+        out_ref[y, 0] = local_ref[y, 0] + entry
+        out_ref[y, 2] = gradient
+        entry = d2 * entry
+    for y in range(half - 1, -1, -1):
+        shifted = local_ref[y, 2]
+        if y == 0:
+            shifted = jnp.where(even, before, shifted)
+        out_ref[y, 1] = (local_ref[y, 1] + after) + shifted
+        after = d2 * after
 
 
 def finish_kernel(got_ref, keep_ref, order_ref, forward_ref, adjoint_ref, gradient_ref):
-    def rows(ref, n):
-        return jnp.concatenate([ref[pl.ds((n * TILES + t) * ROWS, ROWS), :] for t in range(TILES)], 1)
-
-    adjoint = rows(got_ref, 1) + (rows(got_ref, 2) + rows(keep_ref, 0))
-    parts = jnp.concatenate([rows(got_ref, 0), adjoint, rows(got_ref, 3)], 0)
-    parts = reorder(parts, order_ref[...], 0)
+    def rows(n, h):
+        return jnp.concatenate([got_ref[2 * t + h, n] for t in range(TILES)], 1)
+
+    keep = jnp.concatenate([keep_ref[pl.ds(t * ROWS, ROWS), :] for t in range(TILES)], 1)
+    forward, adjoint, gradient = (jnp.concatenate([rows(n, 0), rows(n, 1)], 0) for n in range(3))
+    parts = jnp.concatenate([forward, adjoint + keep, gradient], 0)
+    parts = reorder(parts, order_ref[...])
     forward_ref[...] = parts[0:ROWS]
     adjoint_ref[...] = parts[ROWS : 2 * ROWS]
     gradient_ref[...] = parts[2 * ROWS : 3 * ROWS]
@@ -358,6 +373,10 @@
 
 def in_vmem(count):
     return [pl.BlockSpec(memory_space=pltpu.VMEM)] * count
+
+
+def tiles(*lead):
+    return pltpu.VMEM((*lead, 8, LANES), jnp.float32)
 
 
 def in_place(value):
@@ -385,26 +404,38 @@
         out_shape=(pltpu.VMEM((7, ROWS, COLS), jnp.float32), pltpu.VMEM((COLS, COLS), jnp.bfloat16)),
         in_specs=[pl.BlockSpec(memory_space=pl.ANY)] * 7,
         out_specs=in_vmem(2),
-        scratch_shapes=[pltpu.VMEM((7, ROWS, COLS), jnp.float32), pltpu.SemaphoreType.DMA((7,))],
+        scratch_shapes=[
+            pltpu.VMEM((7, ROWS, COLS), jnp.float32),
+            pltpu.VMEM((COLS, COLS), jnp.bfloat16),
+            pltpu.SemaphoreType.DMA((7,)),
+        ],
         name="pack",
     )(control, initial, diffusion, reaction, forward_guess[0], adjoint_guess[0], observed[0])
     both = in_place(lax.all_gather(own, "space", axis=0))
     own = in_place(own)
     block = jax.ShapeDtypeStruct((ROWS, COLS), jnp.float32)
-    rows = pltpu.VMEM((SLABS, LANES), jnp.float32)
     channels, keep = pl.pallas_call(
         relax_kernel,
-        out_shape=(rows, pltpu.VMEM((64, LANES), jnp.float32)),
+        out_shape=(tiles(8, 4), pltpu.VMEM((64, LANES), jnp.float32)),
         in_specs=in_vmem(2),
         out_specs=in_vmem(2),
         scratch_shapes=relax_scratch(),
         name="relax",
     )(own, both)
-    got = in_place(lax.all_to_all(channels, TM, 0, 0, tiled=True))
+    got = lax.all_to_all(channels, "tm_2", 0, 0, tiled=True)
+    got = in_place(lax.all_gather(got, "tm_3", axis=0))
+    totals, local = pl.pallas_call(
+        block_kernel,
+        out_shape=(tiles(BLOCKS, 4), tiles(8, 3)),
+        in_specs=in_vmem(2),
+        out_specs=in_vmem(2),
+        name="block",
+    )(got, own)
+    totals = in_place(lax.all_to_all(totals, ("tm_0", "tm_1"), 0, 0, tiled=True))
     sent = pl.pallas_call(
-        chain_kernel, out_shape=rows, in_specs=in_vmem(2), out_specs=in_vmem(1)[0], name="chain"
-    )(got, own)
-    back = in_place(lax.all_to_all(sent, TM, 0, 0, tiled=True))
+        spread_kernel, out_shape=tiles(8, 3), in_specs=in_vmem(3), out_specs=in_vmem(1)[0], name="spread"
+    )(totals, in_place(local), own)
+    back = in_place(lax.all_to_all(sent, "tm_2", 0, 0, tiled=True))
     keep, order = in_place(keep), in_place(order)
     forward_states, adjoint_states, gradient = pl.pallas_call(
         finish_kernel, out_shape=(block, block, block), in_specs=in_vmem(3), out_specs=in_vmem(3), name="finish"

time: 73.3 us -> 67.3 us (0.918)
  the two profiles are of different devices: /device:TPU:1 before, /device:TPU:6 now
where the time goes in v5:
time: 67.3 us; the launch traced here: 67 us
  blocking collectives  59.9 us (89%)
  Pallas kernels  6.48 us (10%)
    all_to_all x1, blocking collectives, shards(): lax.all_to_all(totals, ('tm_0', 'tm_1'), 0, 0, tiled=True)  21.3 us
    all_to_all x1, blocking collectives, shards(): got = lax.all_to_all(channels, 'tm_2', 0, 0, tiled=True)  16 us
    all_to_all x1, blocking collectives, shards(): back = in_place(lax.all_to_all(sent, 'tm_2', 0, 0, tiled=True))  11.1 us
    all_gather x1, blocking collectives, shards(): both = in_place(lax.all_gather(own, 'space', axis=0))  9.53 us
    pallas_call x1, Pallas kernels, shards(): pl.pallas_call(relax_kernel, out_shape=(tiles(8, 4), pltpu.VMEM((64, LANE...  4.04 us
    all_gather x1, blocking collectives, shards(): got = in_place(lax.all_gather(got, 'tm_3', axis=0))  1.98 us

profile of v5, /device:TPU:6, one launch (start us, length us, event | category | flops | bytes accessed | tf_op | source)
XLA Modules:
  0.0 67.0 jit_solution(16380805428237028760)
XLA Ops:
  0.6 1.3 %pack.1 = (f32[7,16,512]{2,1,0:T(8,128)S(1)}, bf16[512,512]{1,0:T(8,128)(2,1)S(1)}) custom-call(f32[16,512]{1,0:T(8,128)} %control.1, f32[16,512]{1,0:T(8,128)} %initial.1, f32[16,512]{1,0:T(8,128)} %diffusion.1, f32[16,512]{1,0:T(8,128)} %reaction.1, f32[16,512]{1,0:T(8,128)} %bitcast.9, f32[16,512]{1,0:T(8,128)} %bitcast.10, f32[16,512]{1,0:T(8,128)} %bitcast.11), custom_call_target="tpu_custom_call" | custom-call | tf_op jit(solution)/shard_map/pack/pallas_call | solution.py:402
  2.0 9.5 %all-gather = f32[14,16,512]{2,1,0:T(8,128)S(1)} all-gather(f32[7,16,512]{2,1,0:T(8,128)S(1)} %get-tuple-element.12.own_ref), channel_id=2, replica_groups=mesh['tm_0'=2,'tm_1'=8,'tm_2'=8,'tm_3'=2,'space'=2] {'space'}, dimensions={0}, use_global_device_ids=true | all-gather | bytes 688128 | tf_op jit(solution)/shard_map/all_gather | solution.py:414
  11.5 4.0 %relax.1 = (f32[8,4,8,128]{3,2,1,0:T(8,128)S(1)}, f32[64,128]{1,0:T(8,128)S(1)}) custom-call(f32[7,16,512]{2,1,0:T(8,128)S(1)} %get-tuple-element.12.own_ref, f32[2,7,16,512]{3,2,1,0:T(8,128)S(1)} %bitcast.7), custom_call_target="tpu_custom_call" | custom-call | tf_op jit(solution)/shard_map/relax/pallas_call | solution.py:417
  15.5 16.0 %all_to_all.15 = f32[8,4,8,128]{3,2,1,0:T(8,128)S(1)} all-to-all(f32[8,4,8,128]{3,2,1,0:T(8,128)S(1)} %get-tuple-element.13), channel_id=1, replica_groups=mesh['tm_0'=2,'tm_1'=8,'tm_2'=8,'tm_3'=2,'space'=2] {'tm_2'}, dimensions={0} | all-to-all | bytes 262144 | tf_op jit(solution)/shard_map/all_to_all | solution.py:425
  31.5 2.0 %all-gather.1 = f32[16,4,8,128]{3,2,1,0:T(8,128)S(1)} all-gather(f32[8,4,8,128]{3,2,1,0:T(8,128)S(1)} %all_to_all.15), channel_id=3, replica_groups=mesh['tm_0'=2,'tm_1'=8,'tm_2'=8,'tm_3'=2,'space'=2] {'tm_3'}, dimensions={0}, use_global_device_ids=true | all-gather | bytes 393216 | tf_op jit(solution)/shard_map/all_gather | solution.py:426
  33.5 0.1 block.1
  33.6 21.3 %all_to_all.16.totals_ref = f32[16,4,8,128]{3,2,1,0:T(8,128)S(1)} all-to-all(f32[16,4,8,128]{3,2,1,0:T(8,128)S(1)} %get-tuple-element.14), channel_id=1, replica_groups=mesh['tm_0'=2,'tm_1'=8,'tm_2'=8,'tm_3'=2,'space'=2] {'tm_0','tm_1'}, dimensions={0} | all-to-all | bytes 524288 | tf_op jit(solution)/shard_map/all_to_all | solution.py:434
  54.9 0.1 spread.1
  54.9 11.1 %all_to_all.17.got_ref = f32[8,3,8,128]{3,2,1,0:T(8,128)S(1)} all-to-all(f32[8,3,8,128]{3,2,1,0:T(8,128)S(1)} %spread.1), channel_id=1, replica_groups=mesh['tm_0'=2,'tm_1'=8,'tm_2'=8,'tm_3'=2,'space'=2] {'tm_2'}, dimensions={0} | all-to-all | bytes 196608 | tf_op jit(solution)/shard_map/all_to_all | solution.py:438
  66.0 1.0 %finish.1 = (f32[16,512]{1,0:T(8,128)}, f32[16,512]{1,0:T(8,128)}, f32[16,512]{1,0:T(8,128)}) custom-call(f32[8,3,8,128]{3,2,1,0:T(8,128)S(1)} %all_to_all.17.got_ref, f32[64,128]{1,0:T(8,128)S(1)} %get-tuple-element.16.keep_ref, bf16[512,512]{1,0:T(8,128)(2,1)S(1)} %get-tuple-element.17.order_ref), custom_call_target="tpu_custom_call" | custom-call | tf_op jit(solution)/shard_map/finish/pallas_call | solution.py:440

commit v6 on v5

--- a/solution.py
+++ b/solution.py
@@ -18,8 +18,9 @@
 BLOCK = 16
 BLOCKS = SLABS // BLOCK
 
-ENTRY, FORWARD, ADJOINT, TARGET, CONTROL, SPREAD, REACTION = range(7)
-DAMPING, ALPHA, BETA, GAMMA, SOURCE, STATE, TOTAL, FW_LESS, AD_LESS = range(9)
+FORWARD, ADJOINT, TARGET, CONTROL, SPREAD, REACTION = range(6)
+ARRAYS = 6
+DAMPING, ALPHA, BETA, GAMMA, SOURCE, STATE, TOTAL, FW_LESS, AD_LESS, HEAD, HEAD_ADJOINT = range(11)
 
 
 def tm_index():
@@ -102,22 +103,21 @@
 
 
 def pack_kernel(control, initial, diffusion, reaction, forward, adjoint, observed, out_ref, order_ref, raw, into, sems):
-    is_last = tm_index() == SLABS - 1
+    is_first = tm_index() == 0
 
     def copy(source, slot):
         return pltpu.make_async_copy(source, raw.at[slot], sems.at[slot])
 
-    @pl.when(is_last)
+    @pl.when(is_first)
     def _():
-        copy(initial, ENTRY).start()
-
-    @pl.when(jnp.logical_not(is_last))
+        copy(initial, ADJOINT).start()
+
+    @pl.when(jnp.logical_not(is_first))
     def _():
-        copy(forward, ENTRY).start()
+        copy(adjoint, ADJOINT).start()
 
     rest = (
         (forward, FORWARD),
-        (adjoint, ADJOINT),
         (observed, TARGET),
         (control, CONTROL),
         (diffusion, SPREAD),
@@ -131,27 +131,26 @@
     column, lane = (lax.broadcasted_iota(jnp.int32, (COLS, LANES), d) for d in (0, 1))
     for t in range(TILES):
         into[:, t * LANES : (t + 1) * LANES] = jnp.where(column == TILES * lane + t, 1.0, 0.0).astype(jnp.bfloat16)
-    copy(forward, ENTRY).wait()
+    copy(adjoint, ADJOINT).wait()
     for source, slot in rest:
         copy(source, slot).wait()
-    packed = reorder(raw[...].reshape(7 * ROWS, COLS), into[...])
-    out_ref[...] = packed.reshape(7, ROWS, COLS)
+    packed = reorder(raw[...].reshape(ARRAYS * ROWS, COLS), into[...])
+    out_ref[...] = packed.reshape(ARRAYS, ROWS, COLS)
 
 
 def relax_kernel(own_ref, both_ref, chan_ref, keep_ref, raw, grid, field, wide, points, coarse_points):
     slab = tm_index()
     space = space_index()
     widen, neighbours = make_stencil(space)
-    is_last = slab == SLABS - 1
-    not_last = jnp.where(is_last, 0.0, 1.0)
+    not_last = jnp.where(slab == SLABS - 1, 0.0, 1.0)
     not_first = jnp.where(slab == 0, 0.0, 1.0)
 
-    for n in range(7):
+    for n in range(ARRAYS):
         for t in range(TILES):
             cols = pl.ds(t * LANES, LANES)
             raw[n, t, 0:ROWS, :] = own_ref[n, :, cols]
             raw[n, t, ROWS : 2 * ROWS, :] = both_ref[1 - space, n, :, cols]
-    for n in range(7):
+    for n in range(ARRAYS):
         for p in range(PHASES):
             for t in range(TILES):
                 grid[n, p, t] = raw[n, t, pl.ds(p, 8, stride=PHASES), :]
@@ -186,7 +185,7 @@
         final = neighbours(each(jnp.multiply, weight_wide(1), carried))
         return each(lambda s, i, f: s * i + f, summed, inverse_wide(0), final)
 
-    store(load(grid, ENTRY), field, STATE)
+    store(load(grid, FORWARD), field, STATE)
     store(load(grid, ADJOINT), field, BETA)
     store(each(lambda g: g / COARSEN, load(grid, FORWARD)), field, GAMMA)
 
@@ -202,7 +201,30 @@
 
     lax.fori_loop(0, COARSEN, forward_body, 0)
 
-    forward_less = jnp.where(is_last, SLABS - 1, SLABS - 2 - slab)
+    zeros = each(jnp.zeros_like, damping)
+    store(zeros, field, HEAD)
+    store(zeros, field, HEAD_ADJOINT)
+
+    @pl.when(slab == 0)
+    def _():
+        store(load(grid, ADJOINT), field, HEAD)
+
+        def head_body(i, _):
+            v = forward_step(each(jnp.add, load(field, HEAD), load(grid, CONTROL)))
+            store(v, field, HEAD)
+            store(v, coarse_points, i)
+            return 0
+
+        def head_adjoint_body(n, _):
+            at = COARSEN - 2 - n
+            v = each(lambda a, f: a + f / COARSEN, load(field, HEAD_ADJOINT), load(coarse_points, at))
+            store(adjoint_step(v), field, HEAD_ADJOINT)
+            return 0
+
+        lax.fori_loop(0, COARSEN, head_body, 0)
+        lax.fori_loop(0, COARSEN - 1, head_adjoint_body, 0)
+
+    forward_less = jnp.maximum(SLABS - 2 - slab, 0)
     adjoint_less = jnp.maximum(slab - 1, 0)
     for slot, count in ((FW_LESS, forward_less), (AD_LESS, adjoint_less)):
         power, block = (damping, each(jnp.ones_like, damping))
@@ -215,10 +237,19 @@
                 power = each(lambda q: q * q, power)
         store(total, field, slot)
 
-    push = each(lambda f, d, g: f - not_last * (d * g), load(field, STATE), load(field, DAMPING), load(grid, FORWARD))
+    head = load(field, HEAD)
+    push = each(
+        lambda f, d, g, h: f - d * (g - h), load(field, STATE), load(field, DAMPING), load(grid, FORWARD), head
+    )
     store(push, field, SOURCE)
     store(
-        each(lambda w, u, e: w * u + (1.0 - not_last) * e, load(field, FW_LESS), push, load(grid, ENTRY)),
+        each(
+            lambda w, u, h, e: w * u + (h + (1.0 - not_first) * e),
+            load(field, FW_LESS),
+            push,
+            head,
+            load(grid, ADJOINT),
+        ),
         field,
         STATE,
     )
@@ -237,23 +268,26 @@
 
     damping = load(field, DAMPING)
     alpha, beta, gamma = (load(field, ALPHA), load(field, BETA), load(field, GAMMA))
-    keep = each(lambda g, d, a: g + not_last * (d * a), gamma, damping, alpha)
+    keep = each(
+        lambda g, d, a, h: g + not_last * (d * a) + h, gamma, damping, alpha, load(field, HEAD_ADJOINT)
+    )
     pull = each(lambda k, d, g, b: d * (k - g) + b, keep, damping, load(grid, ADJOINT), beta)
     push = load(field, SOURCE)
     less = load(field, AD_LESS)
     store(
-        each(lambda a, k, w, q, d: a + k + not_first * ((1.0 + d * w) * q), alpha, keep, less, pull, damping),
+        each(lambda a, k, w, q, d: not_last * a + k + not_first * ((1.0 + d * w) * q), alpha, keep, less, pull, damping),
         field,
         TOTAL,
     )
     rest = each(lambda a, k, w, q: not_last * a + not_first * (k + w * q), alpha, keep, less, pull)
     store(
         each(
-            lambda t, w, d, u, o: t + ((1.0 + d * w) * u - o) / COARSEN,
+            lambda t, w, d, u, h, o: t + (not_last * ((1.0 + d * w) * u) + h - o) / COARSEN,
             rest,
             load(field, FW_LESS),
             damping,
             push,
+            load(field, HEAD),
             load(grid, TARGET),
         ),
         field,
@@ -281,9 +315,11 @@
         for t in range(TILES):
             for h in range(2):
                 chan_ref[2 * t + h, n] = raw[n, t, 8 * h : 8 * h + 8, :]
-    for p in range(PHASES):
-        for t in range(TILES):
-            keep_ref[pl.ds(t * ROWS + p, 4, stride=PHASES), :] = field[STATE, p, t, 0:4, :]
+    for n, slot in enumerate((HEAD, STATE)):
+        for p in range(PHASES):
+            for t in range(TILES):
+                at = (n * TILES + t) * ROWS + p
+                keep_ref[pl.ds(at, 4, stride=PHASES), :] = field[slot, p, t, 0:4, :]
 
 
 def owned_damping(own_ref):
@@ -314,12 +350,11 @@
     gradient = [source(3, i) for i in range(BLOCK)]
     while len(gradient) > 1:
         gradient = [a + b for a, b in zip(gradient[::2], gradient[1::2])]
-    first = jnp.where(block == BLOCKS - 1, source(0, BLOCK - 1), forward[BLOCK])
     whole = d * adjoint[0] + source(1, 0)
-    totals = (first, whole, shifted[BLOCK], gradient[0])
     for b in range(BLOCKS):
-        for n, value in enumerate(totals):
-            totals_ref[b, n] = value
+        totals_ref[b, 0] = jnp.where(b > block, forward[BLOCK], whole)
+        totals_ref[b, 1] = shifted[BLOCK]
+        totals_ref[b, 2] = gradient[0]
     for y in range(BLOCK // 2):
         for n, values in enumerate((forward, adjoint, shifted)):
             local_ref[y, n] = jnp.where(even, values[2 * y], values[2 * y + 1])
@@ -332,14 +367,14 @@
     d2 = d * d
     d4 = d2 * d2
     d16 = (d4 * d4) * (d4 * d4)
-    entry = totals_ref[BLOCKS - 1, 0]
+    entry = jnp.zeros_like(d)
     for b in range(BLOCKS - 1):
         entry = jnp.where(b < block, d16 * entry + totals_ref[b, 0], entry)
     after = jnp.zeros_like(d)
     for b in range(BLOCKS - 1, 0, -1):
-        after = jnp.where(b > block, d16 * after + totals_ref[b, 1], after)
-    before = totals_ref[(block + BLOCKS - 1) % BLOCKS, 2]
-    gradient = [totals_ref[b, 3] for b in range(BLOCKS)]
+        after = jnp.where(b > block, d16 * after + totals_ref[b, 0], after)
+    before = jnp.where(block > 0, totals_ref[jnp.maximum(block - 1, 0), 1], 0.0)
+    gradient = [totals_ref[b, 2] for b in range(BLOCKS)]
     while len(gradient) > 1:
         gradient = [a + b for a, b in zip(gradient[::2], gradient[1::2])]
     gradient = gradient[0] * (1.0 / (COARSEN * SLABS))
@@ -362,9 +397,11 @@
     def rows(n, h):
         return jnp.concatenate([got_ref[2 * t + h, n] for t in range(TILES)], 1)
 
-    keep = jnp.concatenate([keep_ref[pl.ds(t * ROWS, ROWS), :] for t in range(TILES)], 1)
+    head, keep = (
+        jnp.concatenate([keep_ref[pl.ds((n * TILES + t) * ROWS, ROWS), :] for t in range(TILES)], 1) for n in range(2)
+    )
     forward, adjoint, gradient = (jnp.concatenate([rows(n, 0), rows(n, 1)], 0) for n in range(3))
-    parts = jnp.concatenate([forward, adjoint + keep, gradient], 0)
+    parts = jnp.concatenate([forward + head, adjoint + keep, gradient], 0)
     parts = reorder(parts, order_ref[...])
     forward_ref[...] = parts[0:ROWS]
     adjoint_ref[...] = parts[ROWS : 2 * ROWS]
@@ -389,25 +426,25 @@
 
 def relax_scratch():
     return [
-        pltpu.VMEM((7, TILES, 2 * ROWS, LANES), jnp.float32),
-        field_shape(7),
-        field_shape(9),
+        pltpu.VMEM((ARRAYS, TILES, 2 * ROWS, LANES), jnp.float32),
+        field_shape(ARRAYS),
+        field_shape(11),
         pltpu.VMEM((2, PHASES, TILES + 2 * SWEEPS, 8, LANES), jnp.float32),
         field_shape(COARSEN),
-        field_shape(COARSEN - 1),
+        field_shape(COARSEN),
     ]
 
 
 def shards(control, initial, diffusion, reaction, forward_guess, adjoint_guess, observed):
     own, order = pl.pallas_call(
         pack_kernel,
-        out_shape=(pltpu.VMEM((7, ROWS, COLS), jnp.float32), pltpu.VMEM((COLS, COLS), jnp.bfloat16)),
+        out_shape=(pltpu.VMEM((ARRAYS, ROWS, COLS), jnp.float32), pltpu.VMEM((COLS, COLS), jnp.bfloat16)),
         in_specs=[pl.BlockSpec(memory_space=pl.ANY)] * 7,
         out_specs=in_vmem(2),
         scratch_shapes=[
-            pltpu.VMEM((7, ROWS, COLS), jnp.float32),
+            pltpu.VMEM((ARRAYS, ROWS, COLS), jnp.float32),
             pltpu.VMEM((COLS, COLS), jnp.bfloat16),
-            pltpu.SemaphoreType.DMA((7,)),
+            pltpu.SemaphoreType.DMA((ARRAYS,)),
         ],
         name="pack",
     )(control, initial, diffusion, reaction, forward_guess[0], adjoint_guess[0], observed[0])
@@ -416,7 +453,7 @@
     block = jax.ShapeDtypeStruct((ROWS, COLS), jnp.float32)
     channels, keep = pl.pallas_call(
         relax_kernel,
-        out_shape=(tiles(8, 4), pltpu.VMEM((64, LANES), jnp.float32)),
+        out_shape=(tiles(8, 4), pltpu.VMEM((128, LANES), jnp.float32)),
         in_specs=in_vmem(2),
         out_specs=in_vmem(2),
         scratch_shapes=relax_scratch(),
@@ -426,7 +463,7 @@
     got = in_place(lax.all_gather(got, "tm_3", axis=0))
     totals, local = pl.pallas_call(
         block_kernel,
-        out_shape=(tiles(BLOCKS, 4), tiles(8, 3)),
+        out_shape=(tiles(BLOCKS, 3), tiles(8, 3)),
         in_specs=in_vmem(2),
         out_specs=in_vmem(2),
         name="block",

time: 67.3 us -> 65.4 us (0.972)
  blocking collectives: 59.9 us -> 58 us
    all_to_all x1, blocking collectives: 21.3 us -> 20.2 us  [shards(): lax.all_to_all(totals, ('tm_0', 'tm_1'), 0, 0, tiled=True)]
    all_gather x1, blocking collectives: 9.53 us -> 8.82 us  [shards(): both = in_place(lax.all_gather(own, 'space', axis=0))]
where the time goes in v6:
time: 65.4 us; the launch traced here: 65.1 us
  blocking collectives  58 us (89%)
  Pallas kernels  6.43 us (10%)
    all_to_all x1, blocking collectives, shards(): lax.all_to_all(totals, ('tm_0', 'tm_1'), 0, 0, tiled=True)  20.2 us
    all_to_all x1, blocking collectives, shards(): got = lax.all_to_all(channels, 'tm_2', 0, 0, tiled=True)  16 us
    all_to_all x1, blocking collectives, shards(): back = in_place(lax.all_to_all(sent, 'tm_2', 0, 0, tiled=True))  11.1 us
    all_gather x1, blocking collectives, shards(): both = in_place(lax.all_gather(own, 'space', axis=0))  8.82 us
    pallas_call x1, Pallas kernels, shards(): pl.pallas_call(relax_kernel, out_shape=(tiles(8, 4), pltpu.VMEM((128, LAN...  4.01 us
    all_gather x1, blocking collectives, shards(): got = in_place(lax.all_gather(got, 'tm_3', axis=0))  1.98 us

profile of v6, /device:TPU:6, one launch (start us, length us, event | category | flops | bytes accessed | tf_op | source)
XLA Modules:
  0.0 65.1 jit_solution(1164273462041717659)
XLA Ops:
  0.6 1.3 %pack.1 = (f32[6,16,512]{2,1,0:T(8,128)S(1)}, bf16[512,512]{1,0:T(8,128)(2,1)S(1)}) custom-call(f32[16,512]{1,0:T(8,128)} %control.1, f32[16,512]{1,0:T(8,128)} %initial.1, f32[16,512]{1,0:T(8,128)} %diffusion.1, f32[16,512]{1,0:T(8,128)} %reaction.1, f32[16,512]{1,0:T(8,128)} %bitcast.9, f32[16,512]{1,0:T(8,128)} %bitcast.10, f32[16,512]{1,0:T(8,128)} %bitcast.11), custom_call_target="tpu_custom_call" | custom-call | tf_op jit(solution)/shard_map/pack/pallas_call | solution.py:439
  1.9 8.8 %all-gather = f32[12,16,512]{2,1,0:T(8,128)S(1)} all-gather(f32[6,16,512]{2,1,0:T(8,128)S(1)} %get-tuple-element.12.own_ref), channel_id=2, replica_groups=mesh['tm_0'=2,'tm_1'=8,'tm_2'=8,'tm_3'=2,'space'=2] {'space'}, dimensions={0}, use_global_device_ids=true | all-gather | bytes 589824 | tf_op jit(solution)/shard_map/all_gather | solution.py:451
  10.8 4.0 %relax.1 = (f32[8,4,8,128]{3,2,1,0:T(8,128)S(1)}, f32[128,128]{1,0:T(8,128)S(1)}) custom-call(f32[6,16,512]{2,1,0:T(8,128)S(1)} %get-tuple-element.12.own_ref, f32[2,6,16,512]{3,2,1,0:T(8,128)S(1)} %bitcast.7), custom_call_target="tpu_custom_call" | custom-call | tf_op jit(solution)/shard_map/relax/pallas_call | solution.py:454
  14.8 16.0 %all_to_all.15 = f32[8,4,8,128]{3,2,1,0:T(8,128)S(1)} all-to-all(f32[8,4,8,128]{3,2,1,0:T(8,128)S(1)} %get-tuple-element.13), channel_id=1, replica_groups=mesh['tm_0'=2,'tm_1'=8,'tm_2'=8,'tm_3'=2,'space'=2] {'tm_2'}, dimensions={0} | all-to-all | bytes 262144 | tf_op jit(solution)/shard_map/all_to_all | solution.py:462
  30.7 2.0 %all-gather.1 = f32[16,4,8,128]{3,2,1,0:T(8,128)S(1)} all-gather(f32[8,4,8,128]{3,2,1,0:T(8,128)S(1)} %all_to_all.15), channel_id=3, replica_groups=mesh['tm_0'=2,'tm_1'=8,'tm_2'=8,'tm_3'=2,'space'=2] {'tm_3'}, dimensions={0}, use_global_device_ids=true | all-gather | bytes 393216 | tf_op jit(solution)/shard_map/all_gather | solution.py:463
  32.7 0.1 block.1
  32.8 20.2 %all_to_all.16.totals_ref = f32[16,3,8,128]{3,2,1,0:T(8,128)S(1)} all-to-all(f32[16,3,8,128]{3,2,1,0:T(8,128)S(1)} %get-tuple-element.14), channel_id=1, replica_groups=mesh['tm_0'=2,'tm_1'=8,'tm_2'=8,'tm_3'=2,'space'=2] {'tm_0','tm_1'}, dimensions={0} | all-to-all | bytes 393216 | tf_op jit(solution)/shard_map/all_to_all | solution.py:471
  52.9 0.1 spread.1
  53.0 11.1 %all_to_all.17.got_ref = f32[8,3,8,128]{3,2,1,0:T(8,128)S(1)} all-to-all(f32[8,3,8,128]{3,2,1,0:T(8,128)S(1)} %spread.1), channel_id=1, replica_groups=mesh['tm_0'=2,'tm_1'=8,'tm_2'=8,'tm_3'=2,'space'=2] {'tm_2'}, dimensions={0} | all-to-all | bytes 196608 | tf_op jit(solution)/shard_map/all_to_all | solution.py:475
  64.1 1.0 %finish.1 = (f32[16,512]{1,0:T(8,128)}, f32[16,512]{1,0:T(8,128)}, f32[16,512]{1,0:T(8,128)}) custom-call(f32[8,3,8,128]{3,2,1,0:T(8,128)S(1)} %all_to_all.17.got_ref, f32[128,128]{1,0:T(8,128)S(1)} %get-tuple-element.16.keep_ref, bf16[512,512]{1,0:T(8,128)(2,1)S(1)} %get-tuple-element.17.order_ref), custom_call_target="tpu_custom_call" | custom-call | tf_op jit(solution)/shard_map/finish/pallas_call | solution.py:477

commit v7 on v6

--- a/solution.py
+++ b/solution.py
@@ -185,21 +185,16 @@
         final = neighbours(each(jnp.multiply, weight_wide(1), carried))
         return each(lambda s, i, f: s * i + f, summed, inverse_wide(0), final)
 
-    store(load(grid, FORWARD), field, STATE)
-    store(load(grid, ADJOINT), field, BETA)
-    store(each(lambda g: g / COARSEN, load(grid, FORWARD)), field, GAMMA)
-
-    def forward_body(i, _):
-        v = forward_step(each(jnp.add, load(field, STATE), load(grid, CONTROL)))
-        beta = adjoint_step(load(field, BETA))
-        gamma = adjoint_step(each(lambda a, o: a - o / COARSEN, load(field, GAMMA), load(grid, TARGET)))
-        store(v, field, STATE)
+    v, beta = (load(grid, FORWARD), load(grid, ADJOINT))
+    gamma = each(lambda g: g / COARSEN, load(grid, FORWARD))
+    for i in range(COARSEN):
+        v = forward_step(each(jnp.add, v, load(grid, CONTROL)))
         store(v, points, i)
-        store(beta, field, BETA)
-        store(gamma, field, GAMMA)
-        return 0
-
-    lax.fori_loop(0, COARSEN, forward_body, 0)
+        beta = adjoint_step(beta)
+        gamma = adjoint_step(each(lambda a, o: a - o / COARSEN, gamma, load(grid, TARGET)))
+    store(v, field, STATE)
+    store(beta, field, BETA)
+    store(gamma, field, GAMMA)
 
     zeros = each(jnp.zeros_like, damping)
     store(zeros, field, HEAD)
@@ -253,18 +248,14 @@
         field,
         STATE,
     )
-    store(each(jnp.zeros_like, push), field, ALPHA)
-
-    def adjoint_body(n, _):
+    v, alpha = (load(field, STATE), None)
+    for n in range(COARSEN - 1):
         at = COARSEN - 2 - n
-        alpha = adjoint_step(each(lambda a, f: a + f / COARSEN, load(field, ALPHA), load(points, at)))
-        v = forward_step(each(jnp.add, load(field, STATE), load(grid, CONTROL)))
-        store(alpha, field, ALPHA)
-        store(v, field, STATE)
+        misfit = each(lambda f: f / COARSEN, load(points, at))
+        alpha = adjoint_step(misfit if alpha is None else each(jnp.add, alpha, misfit))
+        v = forward_step(each(jnp.add, v, load(grid, CONTROL)))
         store(v, coarse_points, n)
-        return 0
-
-    lax.fori_loop(0, COARSEN - 1, adjoint_body, 0, unroll=True)
+    store(alpha, field, ALPHA)
 
     damping = load(field, DAMPING)
     alpha, beta, gamma = (load(field, ALPHA), load(field, BETA), load(field, GAMMA))
@@ -296,16 +287,14 @@
     store(pull, field, BETA)
     store(keep, field, STATE)
 
-    def gradient_body(n, _):
-        v = adjoint_step(load(field, GAMMA))
-        store(each(jnp.add, load(field, TOTAL), v), field, TOTAL)
-        at = COARSEN - 2 - n
-        store(
-            each(lambda a, f, o: a + (f - o) / COARSEN, v, load(coarse_points, at), load(grid, TARGET)), field, GAMMA
-        )
-        return 0
-
-    lax.fori_loop(0, COARSEN - 1, gradient_body, 0, unroll=True)
+    v, total = (load(field, GAMMA), load(field, TOTAL))
+    for n in range(COARSEN - 1):
+        v = adjoint_step(v)
+        total = each(jnp.add, total, v)
+        if n < COARSEN - 2:
+            at = COARSEN - 2 - n
+            v = each(lambda a, f, o: a + (f - o) / COARSEN, v, load(coarse_points, at), load(grid, TARGET))
+    store(total, field, TOTAL)
 
     for n, slot in enumerate((SOURCE, BETA, ALPHA, TOTAL)):
         for p in range(PHASES):

time: 65.4 us -> 65 us (level)
  no operation moved by 1% of the time
where the time goes in v7:
time: 65 us; the launch traced here: 64.7 us
  blocking collectives  58 us (89%)
  Pallas kernels  5.97 us (9%)
  between operations  0.65 us (1%)
    all_to_all x1, blocking collectives, shards(): lax.all_to_all(totals, ('tm_0', 'tm_1'), 0, 0, tiled=True)  20.2 us
    all_to_all x1, blocking collectives, shards(): got = lax.all_to_all(channels, 'tm_2', 0, 0, tiled=True)  16 us
    all_to_all x1, blocking collectives, shards(): back = in_place(lax.all_to_all(sent, 'tm_2', 0, 0, tiled=True))  11.1 us
    all_gather x1, blocking collectives, shards(): both = in_place(lax.all_gather(own, 'space', axis=0))  8.82 us
    pallas_call x1, Pallas kernels, shards(): pl.pallas_call(relax_kernel, out_shape=(tiles(8, 4), pltpu.VMEM((128, LAN...  3.54 us
    all_gather x1, blocking collectives, shards(): got = in_place(lax.all_gather(got, 'tm_3', axis=0))  1.98 us

profile of v7, /device:TPU:6, one launch (start us, length us, event | category | flops | bytes accessed | tf_op | source)
XLA Modules:
  0.0 64.7 jit_solution(7074942612594252451)
XLA Ops:
  0.6 1.3 %pack.1 = (f32[6,16,512]{2,1,0:T(8,128)S(1)}, bf16[512,512]{1,0:T(8,128)(2,1)S(1)}) custom-call(f32[16,512]{1,0:T(8,128)} %control.1, f32[16,512]{1,0:T(8,128)} %initial.1, f32[16,512]{1,0:T(8,128)} %diffusion.1, f32[16,512]{1,0:T(8,128)} %reaction.1, f32[16,512]{1,0:T(8,128)} %bitcast.9, f32[16,512]{1,0:T(8,128)} %bitcast.10, f32[16,512]{1,0:T(8,128)} %bitcast.11), custom_call_target="tpu_custom_call" | custom-call | tf_op jit(solution)/shard_map/pack/pallas_call | solution.py:428
  1.9 8.8 %all-gather = f32[12,16,512]{2,1,0:T(8,128)S(1)} all-gather(f32[6,16,512]{2,1,0:T(8,128)S(1)} %get-tuple-element.12.own_ref), channel_id=2, replica_groups=mesh['tm_0'=2,'tm_1'=8,'tm_2'=8,'tm_3'=2,'space'=2] {'space'}, dimensions={0}, use_global_device_ids=true | all-gather | bytes 589824 | tf_op jit(solution)/shard_map/all_gather | solution.py:440
  10.8 3.5 %relax.1 = (f32[8,4,8,128]{3,2,1,0:T(8,128)S(1)}, f32[128,128]{1,0:T(8,128)S(1)}) custom-call(f32[6,16,512]{2,1,0:T(8,128)S(1)} %get-tuple-element.12.own_ref, f32[2,6,16,512]{3,2,1,0:T(8,128)S(1)} %bitcast.7), custom_call_target="tpu_custom_call" | custom-call | tf_op jit(solution)/shard_map/relax/pallas_call | solution.py:443
  14.3 16.0 %all_to_all.15 = f32[8,4,8,128]{3,2,1,0:T(8,128)S(1)} all-to-all(f32[8,4,8,128]{3,2,1,0:T(8,128)S(1)} %get-tuple-element.13), channel_id=1, replica_groups=mesh['tm_0'=2,'tm_1'=8,'tm_2'=8,'tm_3'=2,'space'=2] {'tm_2'}, dimensions={0} | all-to-all | bytes 262144 | tf_op jit(solution)/shard_map/all_to_all | solution.py:451
  30.3 2.0 %all-gather.1 = f32[16,4,8,128]{3,2,1,0:T(8,128)S(1)} all-gather(f32[8,4,8,128]{3,2,1,0:T(8,128)S(1)} %all_to_all.15), channel_id=3, replica_groups=mesh['tm_0'=2,'tm_1'=8,'tm_2'=8,'tm_3'=2,'space'=2] {'tm_3'}, dimensions={0}, use_global_device_ids=true | all-gather | bytes 393216 | tf_op jit(solution)/shard_map/all_gather | solution.py:452
  32.3 0.1 block.1
  32.3 20.2 %all_to_all.16.totals_ref = f32[16,3,8,128]{3,2,1,0:T(8,128)S(1)} all-to-all(f32[16,3,8,128]{3,2,1,0:T(8,128)S(1)} %get-tuple-element.14), channel_id=1, replica_groups=mesh['tm_0'=2,'tm_1'=8,'tm_2'=8,'tm_3'=2,'space'=2] {'tm_0','tm_1'}, dimensions={0} | all-to-all | bytes 393216 | tf_op jit(solution)/shard_map/all_to_all | solution.py:460
  52.5 0.1 spread.1
  52.6 11.1 %all_to_all.17.got_ref = f32[8,3,8,128]{3,2,1,0:T(8,128)S(1)} all-to-all(f32[8,3,8,128]{3,2,1,0:T(8,128)S(1)} %spread.1), channel_id=1, replica_groups=mesh['tm_0'=2,'tm_1'=8,'tm_2'=8,'tm_3'=2,'space'=2] {'tm_2'}, dimensions={0} | all-to-all | bytes 196608 | tf_op jit(solution)/shard_map/all_to_all | solution.py:464
  63.7 1.0 %finish.1 = (f32[16,512]{1,0:T(8,128)}, f32[16,512]{1,0:T(8,128)}, f32[16,512]{1,0:T(8,128)}) custom-call(f32[8,3,8,128]{3,2,1,0:T(8,128)S(1)} %all_to_all.17.got_ref, f32[128,128]{1,0:T(8,128)S(1)} %get-tuple-element.16.keep_ref, bf16[512,512]{1,0:T(8,128)(2,1)S(1)} %get-tuple-element.17.order_ref), custom_call_target="tpu_custom_call" | custom-call | tf_op jit(solution)/shard_map/finish/pallas_call | solution.py:466

commit v8 on v7

--- a/solution.py
+++ b/solution.py
@@ -51,6 +51,12 @@
     return [row[count : len(row) - count] for row in field]
 
 
+def inside():
+    lane = lax.broadcasted_iota(jnp.int32, (8, LANES), 1)
+    left, right = (jnp.where(lane == edge, 0.0, 1.0) for edge in (0, LANES - 1))
+    return [[left] * SWEEPS + [jnp.ones_like(left)] * TILES + [right] * SWEEPS] * PHASES
+
+
 def make_stencil(space):
     sub = lax.broadcasted_iota(jnp.int32, (8, LANES), 0)
     lane = lax.broadcasted_iota(jnp.int32, (8, LANES), 1)
@@ -58,14 +64,13 @@
     down_ok = sub != 7 - 4 * space
     first, last = (lane == 0, lane == LANES - 1)
 
-    def widen(field, outside_zero):
+    def widen(field):
         out = []
         for row in field:
             left = [pltpu.roll(cell, 1, 1) for cell in row[TILES - SWEEPS :]]
             right = [pltpu.roll(cell, LANES - 1, 1) for cell in row[:SWEEPS]]
-            if outside_zero:
-                left = [jnp.where(first, 0.0, cell) for cell in left]
-                right = [jnp.where(last, 0.0, cell) for cell in right]
+            left[-1] = jnp.where(first, 0.0, left[-1])
+            right[0] = jnp.where(last, 0.0, right[0])
             out.append(left + row + right)
         return out
 
@@ -157,8 +162,8 @@
 
     spread, reaction = (load(grid, SPREAD), load(grid, REACTION))
     inverse = each(lambda s, r: 1.0 / (1.0 + 4.0 * s + r), spread, reaction)
-    store(widen(inverse, True), wide, 0)
-    store(widen(each(jnp.multiply, spread, inverse), True), wide, 1)
+    store(each(jnp.multiply, inside(), widen(inverse)), wide, 0)
+    store(each(jnp.multiply, inside(), widen(each(jnp.multiply, spread, inverse))), wide, 1)
     damping = each(lambda r: 1.0 / (1.0 + COARSEN * r), reaction)
     store(damping, field, DAMPING)
 
@@ -169,7 +174,7 @@
         return [[wide[1, p, t] for t in range(SWEEPS - count, SWEEPS + TILES + count)] for p in range(PHASES)]
 
     def forward_step(right_side):
-        v = widen(right_side, True)
+        v = widen(right_side)
         scaled = each(jnp.multiply, inverse_wide(SWEEPS - 1), trim(v, 1))
         for n in range(SWEEPS):
             v = each(
@@ -178,11 +183,12 @@
         return v
 
     def adjoint_step(y):
-        carried, summed = (widen(y, False), y)
+        carried, summed = (widen(each(jnp.multiply, weight_wide(0), y)), y)
         for n in range(SWEEPS - 1):
-            carried = neighbours(each(jnp.multiply, weight_wide(SWEEPS - n), carried))
+            carried = neighbours(carried)
             summed = each(jnp.add, summed, trim(carried, SWEEPS - 1 - n))
-        final = neighbours(each(jnp.multiply, weight_wide(1), carried))
+            carried = each(jnp.multiply, weight_wide(SWEEPS - 1 - n), carried)
+        final = neighbours(carried)
         return each(lambda s, i, f: s * i + f, summed, inverse_wide(0), final)
 
     v, beta = (load(grid, FORWARD), load(grid, ADJOINT))

time: 65 us -> 64.9 us (level)
  no operation moved by 1% of the time
where the time goes in v8:
time: 64.9 us; the launch traced here: 64.6 us
  blocking collectives  58 us (89%)
  Pallas kernels  5.95 us (9%)
  between operations  0.65 us (1%)
    all_to_all x1, blocking collectives, shards(): lax.all_to_all(totals, ('tm_0', 'tm_1'), 0, 0, tiled=True)  20.2 us
    all_to_all x1, blocking collectives, shards(): got = lax.all_to_all(channels, 'tm_2', 0, 0, tiled=True)  16 us
    all_to_all x1, blocking collectives, shards(): back = in_place(lax.all_to_all(sent, 'tm_2', 0, 0, tiled=True))  11.1 us
    all_gather x1, blocking collectives, shards(): both = in_place(lax.all_gather(own, 'space', axis=0))  8.82 us
    pallas_call x1, Pallas kernels, shards(): pl.pallas_call(relax_kernel, out_shape=(tiles(8, 4), pltpu.VMEM((128, LAN...  3.52 us
    all_gather x1, blocking collectives, shards(): got = in_place(lax.all_gather(got, 'tm_3', axis=0))  1.98 us

profile of v8, /device:TPU:6, one launch (start us, length us, event | category | flops | bytes accessed | tf_op | source)
XLA Modules:
  0.0 64.6 jit_solution(15007365576882626114)
XLA Ops:
  0.6 1.3 %pack.1 = (f32[6,16,512]{2,1,0:T(8,128)S(1)}, bf16[512,512]{1,0:T(8,128)(2,1)S(1)}) custom-call(f32[16,512]{1,0:T(8,128)} %control.1, f32[16,512]{1,0:T(8,128)} %initial.1, f32[16,512]{1,0:T(8,128)} %diffusion.1, f32[16,512]{1,0:T(8,128)} %reaction.1, f32[16,512]{1,0:T(8,128)} %bitcast.9, f32[16,512]{1,0:T(8,128)} %bitcast.10, f32[16,512]{1,0:T(8,128)} %bitcast.11), custom_call_target="tpu_custom_call" | custom-call | tf_op jit(solution)/shard_map/pack/pallas_call | solution.py:434
  1.9 8.8 %all-gather = f32[12,16,512]{2,1,0:T(8,128)S(1)} all-gather(f32[6,16,512]{2,1,0:T(8,128)S(1)} %get-tuple-element.12.own_ref), channel_id=2, replica_groups=mesh['tm_0'=2,'tm_1'=8,'tm_2'=8,'tm_3'=2,'space'=2] {'space'}, dimensions={0}, use_global_device_ids=true | all-gather | bytes 589824 | tf_op jit(solution)/shard_map/all_gather | solution.py:446
  10.8 3.5 %relax.1 = (f32[8,4,8,128]{3,2,1,0:T(8,128)S(1)}, f32[128,128]{1,0:T(8,128)S(1)}) custom-call(f32[6,16,512]{2,1,0:T(8,128)S(1)} %get-tuple-element.12.own_ref, f32[2,6,16,512]{3,2,1,0:T(8,128)S(1)} %bitcast.7), custom_call_target="tpu_custom_call" | custom-call | tf_op jit(solution)/shard_map/relax/pallas_call | solution.py:449
  14.3 16.0 %all_to_all.15 = f32[8,4,8,128]{3,2,1,0:T(8,128)S(1)} all-to-all(f32[8,4,8,128]{3,2,1,0:T(8,128)S(1)} %get-tuple-element.13), channel_id=1, replica_groups=mesh['tm_0'=2,'tm_1'=8,'tm_2'=8,'tm_3'=2,'space'=2] {'tm_2'}, dimensions={0} | all-to-all | bytes 262144 | tf_op jit(solution)/shard_map/all_to_all | solution.py:457
  30.3 2.0 %all-gather.1 = f32[16,4,8,128]{3,2,1,0:T(8,128)S(1)} all-gather(f32[8,4,8,128]{3,2,1,0:T(8,128)S(1)} %all_to_all.15), channel_id=3, replica_groups=mesh['tm_0'=2,'tm_1'=8,'tm_2'=8,'tm_3'=2,'space'=2] {'tm_3'}, dimensions={0}, use_global_device_ids=true | all-gather | bytes 393216 | tf_op jit(solution)/shard_map/all_gather | solution.py:458
  32.2 0.1 block.1
  32.3 20.2 %all_to_all.16.totals_ref = f32[16,3,8,128]{3,2,1,0:T(8,128)S(1)} all-to-all(f32[16,3,8,128]{3,2,1,0:T(8,128)S(1)} %get-tuple-element.14), channel_id=1, replica_groups=mesh['tm_0'=2,'tm_1'=8,'tm_2'=8,'tm_3'=2,'space'=2] {'tm_0','tm_1'}, dimensions={0} | all-to-all | bytes 393216 | tf_op jit(solution)/shard_map/all_to_all | solution.py:466
  52.5 0.1 spread.1
  52.5 11.1 %all_to_all.17.got_ref = f32[8,3,8,128]{3,2,1,0:T(8,128)S(1)} all-to-all(f32[8,3,8,128]{3,2,1,0:T(8,128)S(1)} %spread.1), channel_id=1, replica_groups=mesh['tm_0'=2,'tm_1'=8,'tm_2'=8,'tm_3'=2,'space'=2] {'tm_2'}, dimensions={0} | all-to-all | bytes 196608 | tf_op jit(solution)/shard_map/all_to_all | solution.py:470
  63.6 1.0 %finish.1 = (f32[16,512]{1,0:T(8,128)}, f32[16,512]{1,0:T(8,128)}, f32[16,512]{1,0:T(8,128)}) custom-call(f32[8,3,8,128]{3,2,1,0:T(8,128)S(1)} %all_to_all.17.got_ref, f32[128,128]{1,0:T(8,128)S(1)} %get-tuple-element.16.keep_ref, bf16[512,512]{1,0:T(8,128)(2,1)S(1)} %get-tuple-element.17.order_ref), custom_call_target="tpu_custom_call" | custom-call | tf_op jit(solution)/shard_map/finish/pallas_call | solution.py:472

commit v9 on v8

--- a/solution.py
+++ b/solution.py
@@ -191,6 +191,29 @@
         final = neighbours(carried)
         return each(lambda s, i, f: s * i + f, summed, inverse_wide(0), final)
 
+    zeros = each(jnp.zeros_like, damping)
+    store(zeros, field, HEAD)
+    store(zeros, field, HEAD_ADJOINT)
+
+    @pl.when(slab == 0)
+    def _():
+        store(load(grid, ADJOINT), field, HEAD)
+
+        def head_body(i, _):
+            v = forward_step(each(jnp.add, load(field, HEAD), load(grid, CONTROL)))
+            store(v, field, HEAD)
+            store(v, coarse_points, i)
+            return 0
+
+        def head_adjoint_body(n, _):
+            at = COARSEN - 2 - n
+            v = each(lambda a, f: a + f / COARSEN, load(field, HEAD_ADJOINT), load(coarse_points, at))
+            store(adjoint_step(v), field, HEAD_ADJOINT)
+            return 0
+
+        lax.fori_loop(0, COARSEN, head_body, 0)
+        lax.fori_loop(0, COARSEN - 1, head_adjoint_body, 0)
+
     v, beta = (load(grid, FORWARD), load(grid, ADJOINT))
     gamma = each(lambda g: g / COARSEN, load(grid, FORWARD))
     for i in range(COARSEN):
@@ -202,41 +225,20 @@
     store(beta, field, BETA)
     store(gamma, field, GAMMA)
 
-    zeros = each(jnp.zeros_like, damping)
-    store(zeros, field, HEAD)
-    store(zeros, field, HEAD_ADJOINT)
-
-    @pl.when(slab == 0)
-    def _():
-        store(load(grid, ADJOINT), field, HEAD)
-
-        def head_body(i, _):
-            v = forward_step(each(jnp.add, load(field, HEAD), load(grid, CONTROL)))
-            store(v, field, HEAD)
-            store(v, coarse_points, i)
-            return 0
-
-        def head_adjoint_body(n, _):
-            at = COARSEN - 2 - n
-            v = each(lambda a, f: a + f / COARSEN, load(field, HEAD_ADJOINT), load(coarse_points, at))
-            store(adjoint_step(v), field, HEAD_ADJOINT)
-            return 0
-
-        lax.fori_loop(0, COARSEN, head_body, 0)
-        lax.fori_loop(0, COARSEN - 1, head_adjoint_body, 0)
-
     forward_less = jnp.maximum(SLABS - 2 - slab, 0)
     adjoint_less = jnp.maximum(slab - 1, 0)
-    for slot, count in ((FW_LESS, forward_less), (AD_LESS, adjoint_less)):
-        power, block = (damping, each(jnp.ones_like, damping))
-        total = each(jnp.zeros_like, damping)
-        for b in range(8):
+    counts = (forward_less, adjoint_less)
+    power, block = (damping, each(jnp.ones_like, damping))
+    sums = [each(jnp.zeros_like, damping) for _ in counts]
+    for b in range(8):
+        for n, count in enumerate(counts):
             taken = ((count >> b) & 1) == 1
-            total = each(lambda s, v, q: jnp.where(taken, v + q * s, s), total, block, power)
-            if b < 7:
-                block = each(lambda v, q: v + v * q, block, power)
-                power = each(lambda q: q * q, power)
-        store(total, field, slot)
+            sums[n] = each(lambda s, v, q: jnp.where(taken, v + q * s, s), sums[n], block, power)
+        if b < 7:
+            block = each(lambda v, q: v + v * q, block, power)
+            power = each(lambda q: q * q, power)
+    store(sums[0], field, FW_LESS)
+    store(sums[1], field, AD_LESS)
 
     head = load(field, HEAD)
     push = each(

time: 64.9 us -> 65 us (level)
  no operation moved by 1% of the time
where the time goes in v9:
time: 65 us; the launch traced here: 64.7 us
  blocking collectives  58 us (89%)
  Pallas kernels  6.02 us (9%)
  between operations  0.65 us (1%)
    all_to_all x1, blocking collectives, shards(): lax.all_to_all(totals, ('tm_0', 'tm_1'), 0, 0, tiled=True)  20.2 us
    all_to_all x1, blocking collectives, shards(): got = lax.all_to_all(channels, 'tm_2', 0, 0, tiled=True)  16 us
    all_to_all x1, blocking collectives, shards(): back = in_place(lax.all_to_all(sent, 'tm_2', 0, 0, tiled=True))  11.1 us
    all_gather x1, blocking collectives, shards(): both = in_place(lax.all_gather(own, 'space', axis=0))  8.82 us
    pallas_call x1, Pallas kernels, shards(): pl.pallas_call(relax_kernel, out_shape=(tiles(8, 4), pltpu.VMEM((128, LAN...  3.59 us
    all_gather x1, blocking collectives, shards(): got = in_place(lax.all_gather(got, 'tm_3', axis=0))  1.98 us

profile of v9, /device:TPU:6, one launch (start us, length us, event | category | flops | bytes accessed | tf_op | source)
XLA Modules:
  0.0 64.7 jit_solution(1129722534915966691)
XLA Ops:
  0.6 1.3 %pack.1 = (f32[6,16,512]{2,1,0:T(8,128)S(1)}, bf16[512,512]{1,0:T(8,128)(2,1)S(1)}) custom-call(f32[16,512]{1,0:T(8,128)} %control.1, f32[16,512]{1,0:T(8,128)} %initial.1, f32[16,512]{1,0:T(8,128)} %diffusion.1, f32[16,512]{1,0:T(8,128)} %reaction.1, f32[16,512]{1,0:T(8,128)} %bitcast.9, f32[16,512]{1,0:T(8,128)} %bitcast.10, f32[16,512]{1,0:T(8,128)} %bitcast.11), custom_call_target="tpu_custom_call" | custom-call | tf_op jit(solution)/shard_map/pack/pallas_call | solution.py:436
  1.9 8.8 %all-gather = f32[12,16,512]{2,1,0:T(8,128)S(1)} all-gather(f32[6,16,512]{2,1,0:T(8,128)S(1)} %get-tuple-element.12.own_ref), channel_id=2, replica_groups=mesh['tm_0'=2,'tm_1'=8,'tm_2'=8,'tm_3'=2,'space'=2] {'space'}, dimensions={0}, use_global_device_ids=true | all-gather | bytes 589824 | tf_op jit(solution)/shard_map/all_gather | solution.py:448
  10.8 3.6 %relax.1 = (f32[8,4,8,128]{3,2,1,0:T(8,128)S(1)}, f32[128,128]{1,0:T(8,128)S(1)}) custom-call(f32[6,16,512]{2,1,0:T(8,128)S(1)} %get-tuple-element.12.own_ref, f32[2,6,16,512]{3,2,1,0:T(8,128)S(1)} %bitcast.7), custom_call_target="tpu_custom_call" | custom-call | tf_op jit(solution)/shard_map/relax/pallas_call | solution.py:451
  14.4 16.0 %all_to_all.15 = f32[8,4,8,128]{3,2,1,0:T(8,128)S(1)} all-to-all(f32[8,4,8,128]{3,2,1,0:T(8,128)S(1)} %get-tuple-element.13), channel_id=1, replica_groups=mesh['tm_0'=2,'tm_1'=8,'tm_2'=8,'tm_3'=2,'space'=2] {'tm_2'}, dimensions={0} | all-to-all | bytes 262144 | tf_op jit(solution)/shard_map/all_to_all | solution.py:459
  30.3 2.0 %all-gather.1 = f32[16,4,8,128]{3,2,1,0:T(8,128)S(1)} all-gather(f32[8,4,8,128]{3,2,1,0:T(8,128)S(1)} %all_to_all.15), channel_id=3, replica_groups=mesh['tm_0'=2,'tm_1'=8,'tm_2'=8,'tm_3'=2,'space'=2] {'tm_3'}, dimensions={0}, use_global_device_ids=true | all-gather | bytes 393216 | tf_op jit(solution)/shard_map/all_gather | solution.py:460
  32.3 0.1 block.1
  32.4 20.2 %all_to_all.16.totals_ref = f32[16,3,8,128]{3,2,1,0:T(8,128)S(1)} all-to-all(f32[16,3,8,128]{3,2,1,0:T(8,128)S(1)} %get-tuple-element.14), channel_id=1, replica_groups=mesh['tm_0'=2,'tm_1'=8,'tm_2'=8,'tm_3'=2,'space'=2] {'tm_0','tm_1'}, dimensions={0} | all-to-all | bytes 393216 | tf_op jit(solution)/shard_map/all_to_all | solution.py:468
  52.5 0.1 spread.1
  52.6 11.1 %all_to_all.17.got_ref = f32[8,3,8,128]{3,2,1,0:T(8,128)S(1)} all-to-all(f32[8,3,8,128]{3,2,1,0:T(8,128)S(1)} %spread.1), channel_id=1, replica_groups=mesh['tm_0'=2,'tm_1'=8,'tm_2'=8,'tm_3'=2,'space'=2] {'tm_2'}, dimensions={0} | all-to-all | bytes 196608 | tf_op jit(solution)/shard_map/all_to_all | solution.py:472
  63.7 1.0 %finish.1 = (f32[16,512]{1,0:T(8,128)}, f32[16,512]{1,0:T(8,128)}, f32[16,512]{1,0:T(8,128)}) custom-call(f32[8,3,8,128]{3,2,1,0:T(8,128)S(1)} %all_to_all.17.got_ref, f32[128,128]{1,0:T(8,128)S(1)} %get-tuple-element.16.keep_ref, bf16[512,512]{1,0:T(8,128)(2,1)S(1)} %get-tuple-element.17.order_ref), custom_call_target="tpu_custom_call" | custom-call | tf_op jit(solution)/shard_map/finish/pallas_call | solution.py:474

commit v10 on v8

--- a/solution.py
+++ b/solution.py
@@ -100,10 +100,9 @@
 
 
 def reorder(value, selection):
-    high, middle, low = (
-        jnp.dot(term, selection, preferred_element_type=jnp.float32)
-        for term in exact_terms(value)
-    )
+    count = value.shape[0]
+    terms = jnp.dot(jnp.concatenate(exact_terms(value), 0), selection, preferred_element_type=jnp.float32)
+    high, middle, low = (terms[n * count : (n + 1) * count] for n in range(3))
     return high + (middle + low)
 
 

time: 64.9 us -> 64.7 us (level)
  no operation moved by 1% of the time
where the time goes in v10:
time: 64.7 us; the launch traced here: 64.5 us
  blocking collectives  58 us (90%)
  Pallas kernels  5.76 us (9%)
  between operations  0.65 us (1%)
    all_to_all x1, blocking collectives, shards(): lax.all_to_all(totals, ('tm_0', 'tm_1'), 0, 0, tiled=True)  20.2 us
    all_to_all x1, blocking collectives, shards(): got = lax.all_to_all(channels, 'tm_2', 0, 0, tiled=True)  16 us
    all_to_all x1, blocking collectives, shards(): back = in_place(lax.all_to_all(sent, 'tm_2', 0, 0, tiled=True))  11.1 us
    all_gather x1, blocking collectives, shards(): both = in_place(lax.all_gather(own, 'space', axis=0))  8.82 us
    pallas_call x1, Pallas kernels, shards(): pl.pallas_call(relax_kernel, out_shape=(tiles(8, 4), pltpu.VMEM((128, LAN...  3.52 us
    all_gather x1, blocking collectives, shards(): got = in_place(lax.all_gather(got, 'tm_3', axis=0))  1.98 us

profile of v10, /device:TPU:6, one launch (start us, length us, event | category | flops | bytes accessed | tf_op | source)
XLA Modules:
  0.0 64.5 jit_solution(12127091306027435246)
XLA Ops:
  0.6 1.2 %pack.1 = (f32[6,16,512]{2,1,0:T(8,128)S(1)}, bf16[512,512]{1,0:T(8,128)(2,1)S(1)}) custom-call(f32[16,512]{1,0:T(8,128)} %control.1, f32[16,512]{1,0:T(8,128)} %initial.1, f32[16,512]{1,0:T(8,128)} %diffusion.1, f32[16,512]{1,0:T(8,128)} %reaction.1, f32[16,512]{1,0:T(8,128)} %bitcast.9, f32[16,512]{1,0:T(8,128)} %bitcast.10, f32[16,512]{1,0:T(8,128)} %bitcast.11), custom_call_target="tpu_custom_call" | custom-call | tf_op jit(solution)/shard_map/pack/pallas_call | solution.py:433
  1.9 8.8 %all-gather = f32[12,16,512]{2,1,0:T(8,128)S(1)} all-gather(f32[6,16,512]{2,1,0:T(8,128)S(1)} %get-tuple-element.12.own_ref), channel_id=2, replica_groups=mesh['tm_0'=2,'tm_1'=8,'tm_2'=8,'tm_3'=2,'space'=2] {'space'}, dimensions={0}, use_global_device_ids=true | all-gather | bytes 589824 | tf_op jit(solution)/shard_map/all_gather | solution.py:445
  10.7 3.5 %relax.1 = (f32[8,4,8,128]{3,2,1,0:T(8,128)S(1)}, f32[128,128]{1,0:T(8,128)S(1)}) custom-call(f32[6,16,512]{2,1,0:T(8,128)S(1)} %get-tuple-element.12.own_ref, f32[2,6,16,512]{3,2,1,0:T(8,128)S(1)} %bitcast.7), custom_call_target="tpu_custom_call" | custom-call | tf_op jit(solution)/shard_map/relax/pallas_call | solution.py:448
  14.2 16.0 %all_to_all.15 = f32[8,4,8,128]{3,2,1,0:T(8,128)S(1)} all-to-all(f32[8,4,8,128]{3,2,1,0:T(8,128)S(1)} %get-tuple-element.13), channel_id=1, replica_groups=mesh['tm_0'=2,'tm_1'=8,'tm_2'=8,'tm_3'=2,'space'=2] {'tm_2'}, dimensions={0} | all-to-all | bytes 262144 | tf_op jit(solution)/shard_map/all_to_all | solution.py:456
  30.2 2.0 %all-gather.1 = f32[16,4,8,128]{3,2,1,0:T(8,128)S(1)} all-gather(f32[8,4,8,128]{3,2,1,0:T(8,128)S(1)} %all_to_all.15), channel_id=3, replica_groups=mesh['tm_0'=2,'tm_1'=8,'tm_2'=8,'tm_3'=2,'space'=2] {'tm_3'}, dimensions={0}, use_global_device_ids=true | all-gather | bytes 393216 | tf_op jit(solution)/shard_map/all_gather | solution.py:457
  32.2 0.1 block.1
  32.2 20.2 %all_to_all.16.totals_ref = f32[16,3,8,128]{3,2,1,0:T(8,128)S(1)} all-to-all(f32[16,3,8,128]{3,2,1,0:T(8,128)S(1)} %get-tuple-element.14), channel_id=1, replica_groups=mesh['tm_0'=2,'tm_1'=8,'tm_2'=8,'tm_3'=2,'space'=2] {'tm_0','tm_1'}, dimensions={0} | all-to-all | bytes 393216 | tf_op jit(solution)/shard_map/all_to_all | solution.py:465
  52.4 0.1 spread.1
  52.5 11.1 %all_to_all.17.got_ref = f32[8,3,8,128]{3,2,1,0:T(8,128)S(1)} all-to-all(f32[8,3,8,128]{3,2,1,0:T(8,128)S(1)} %spread.1), channel_id=1, replica_groups=mesh['tm_0'=2,'tm_1'=8,'tm_2'=8,'tm_3'=2,'space'=2] {'tm_2'}, dimensions={0} | all-to-all | bytes 196608 | tf_op jit(solution)/shard_map/all_to_all | solution.py:469
  63.6 0.9 %finish.1 = (f32[16,512]{1,0:T(8,128)}, f32[16,512]{1,0:T(8,128)}, f32[16,512]{1,0:T(8,128)}) custom-call(f32[8,3,8,128]{3,2,1,0:T(8,128)S(1)} %all_to_all.17.got_ref, f32[128,128]{1,0:T(8,128)S(1)} %get-tuple-element.16.keep_ref, bf16[512,512]{1,0:T(8,128)(2,1)S(1)} %get-tuple-element.17.order_ref), custom_call_target="tpu_custom_call" | custom-call | tf_op jit(solution)/shard_map/finish/pallas_call | solution.py:471
